TPU v7x, 768 devices: a whole 4x8x12 slice. The times are simulated.
768 devices in a mesh: dom: 96 (over y, z), feat: 8 (over x, core).
Axes of the slice: x: 4, y: 8, z: 12, core: 2. Of those that a mesh axis runs over, the one named last changes fastest.
Arguments:
- features: bfloat16 [98304, 512], P('dom', 'feat'), may hold values from -6 to 6
- w_self: bfloat16 [512, 512], P('feat'), may hold values from -0.25 to 0.25
- w_neigh: bfloat16 [512, 512], P('feat'), may hold values from -0.25 to 0.25
- degree: int32 [98304], P('dom'), may hold values from 1 to 32
- local_vals: bfloat16 [96, 16, 128, 128], P('dom'), may hold values from 0 to 0.19921875
- local_dst: int32 [96, 16], P('dom'), may hold values from 0 to 7
- local_src: int32 [96, 16], P('dom'), may hold values from 0 to 7
- remote_vals: bfloat16 [96, 6, 8, 128, 128], P('dom'), may hold values from 0 to 0.19921875
- remote_dst: int32 [96, 6, 8], P('dom'), may hold values from 0 to 7
- remote_src: int32 [96, 6, 8], P('dom'), may hold values from 0 to 7
- cotangent: bfloat16 [98304, 512], P('dom', 'feat'), may hold values from -6 to 6
Outputs:
- out: bfloat16 [98304, 512], P('dom', 'feat')
- grad_x: float32 [98304, 512], P('dom', 'feat')
- grad_self: float32 [512, 512], P('feat')
- grad_neigh: float32 [512, 512], P('feat')
All inputs are finite; a program needn't handle non-finite values.
Results may differ from a plain program's by a relative error of at most 0.0068.
Values may be sent and summed in bfloat16 or wider, within the bound.
A program may use at most 32 MiB of HBM per device.

v0:
```python
import jax
import jax.numpy as jnp
from jax import lax
from jax.sharding import PartitionSpec as P


def shifted(x, axis, by):
    devices = lax.axis_size(axis)
    return lax.ppermute(x, axis, [(i, (i + by) % devices) for i in range(devices)])


def spread(parts, block_ids, count):
    table = (block_ids[:, None] == jnp.arange(count, dtype=jnp.int32)[None, :]).astype(jnp.float32)
    return jnp.einsum("kc,kif->cif", table, parts, precision=lax.Precision.HIGHEST)


def tile_apply(tiles, blocks):
    return jnp.einsum("kij,kjf->kif", tiles, blocks, preferred_element_type=jnp.float32)


def tile_apply_back(tiles, blocks):
    return jnp.einsum("kji,kjf->kif", tiles, blocks, preferred_element_type=jnp.float32)


def make_back_piece(weights, stacked):

    def back_piece(carry, piece, start):
        dz_acc = lax.dot_general(
            piece, weights, (((1,), (1,)), ((), ())), preferred_element_type=jnp.float32
        )
        product = lax.dot_general(
            stacked, piece, (((0,), (0,)), ((), ())), preferred_element_type=jnp.float32
        )
        return (dz_acc, product)

    return back_piece


def body(
    features,
    w_self,
    w_neigh,
    degree,
    local_vals,
    local_dst,
    local_src,
    remote_vals,
    remote_dst,
    remote_src,
    cotangent,
):
    rows = features.shape[0]
    width = features.shape[1]
    block = local_vals.shape[-1]
    nblocks = rows // block
    rounds = remote_vals.shape[1]
    parts_total = lax.axis_size("dom")
    offsets = [(step + 1) * parts_total // (rounds + 1) for step in range(rounds)]
    blocks = features.reshape(nblocks, block, width)
    totals = spread(
        tile_apply(local_vals[0], jnp.take(blocks, local_src[0], axis=0)), local_dst[0], nblocks
    )
    arrived_ids = []
    for step in range(rounds):
        partial_blocks = tile_apply(
            remote_vals[0, step], jnp.take(blocks, remote_src[0, step], axis=0)
        ).astype(jnp.bfloat16)
        arrived, block_ids = shifted((partial_blocks, remote_dst[0, step]), "dom", offsets[step])
        arrived_ids.append(block_ids)
        totals = totals + spread(arrived.astype(jnp.float32), block_ids, nblocks)
    inverse = 1.0 / degree.astype(jnp.float32)
    agg = (totals.reshape(rows, width) * inverse[:, None]).astype(jnp.bfloat16)
    stacked = jnp.concatenate([features, agg], axis=1)
    weights = jnp.concatenate([w_self, w_neigh], axis=0)
    start_carry = (
        jnp.zeros((rows, 2 * width), jnp.float32),
        jnp.zeros((2 * width, weights.shape[1]), jnp.float32),
    )
    back_piece = make_back_piece(weights, stacked)
    pre = lax.psum_scatter(
        lax.dot_general(
            weights, stacked, (((0,), (1,)), ((), ())), preferred_element_type=jnp.float32
        ),
        "feat",
        scatter_dimension=0,
        tiled=True,
    ).T
    sigma = jax.nn.sigmoid(pre)
    out = (pre * sigma).astype(jnp.bfloat16)
    dpre = (cotangent.astype(jnp.float32) * sigma * (1.0 + pre * (1.0 - sigma))).astype(
        jnp.bfloat16
    )
    dz_total, grad_local = back_piece(
        start_carry, lax.all_gather(dpre, "feat", axis=1, tiled=True), jnp.int32(0)
    )
    dx_self = dz_total[:, :width]
    dsum = (
        (dz_total[:, width:] * inverse[:, None]).astype(jnp.bfloat16).reshape(nblocks, block, width)
    )
    grad_all = lax.psum(grad_local, "dom")
    back = spread(
        tile_apply_back(local_vals[0], jnp.take(dsum, local_dst[0], axis=0)), local_src[0], nblocks
    )
    for step in range(rounds):
        picked = jnp.take(dsum, arrived_ids[step], axis=0)
        returned = shifted(picked, "dom", parts_total - offsets[step])
        back = back + spread(
            tile_apply_back(remote_vals[0, step], returned), remote_src[0, step], nblocks
        )
    grad_x = dx_self + back.reshape(rows, width)
    return (out, grad_x, grad_all[:width], grad_all[width:])


def solution(mesh):
    placed = (
        P("dom", "feat"),
        P("feat", None),
        P("feat", None),
        P("dom"),
        P("dom", None, None, None),
        P("dom", None),
        P("dom", None),
        P("dom", None, None, None, None),
        P("dom", None, None),
        P("dom", None, None),
        P("dom", "feat"),
    )
    return jax.shard_map(
        body,
        mesh=mesh,
        in_specs=placed,
        out_specs=(P("dom", "feat"), P("dom", "feat"), P("feat", None), P("feat", None)),
        check_vma=False,
    )
```

profile of v0, /device:TPU:1, one launch (start us, length us, event | category | flops | bytes accessed | tf_op | source)
XLA Modules:
  0.0 449.3 jit_solution(10302077569670767671)
XLA Ops:
  7.2 1.1 copy_bitcast_fusion.1
  8.3 0.8 compare_and_fusion.11
  9.1 0.6 gather_fusion.6
  9.7 1.3 fusion.9
  10.9 18.8 %collective-permute-start.11 = (bf16[8,128,64]{1,2,0:T(8,128)(2,1)S(1)}, bf16[8,128,64]{1,2,0:T(8,128)(2,1)S(1)}, u32[]{:S(2)}, u32[]{:S(2)}) collective-permute-start(bf16[8,128,64]{1,2,0:T(8,128)(2,1)S(1)} %fusion.9), channel_id=1, source_target_pairs={{0,656},{8,664},{16,672},{24,680},{32,688},{40,696},{48,704},{56,7... | collective-permute-start | bytes 393224 | tf_op jit(solution)/shard_map/ppermute | solution.py:9
  29.8 0.7 slice_bitcast_fusion.9
  30.5 2.9 collective-permute-start.10
  33.5 0.6 gather_fusion.5
  34.1 1.0 fusion.8
  35.1 3.3 collective-permute-start.9
  38.4 0.6 gather_fusion.1
  39.0 1.0 fusion.4
  39.9 3.8 collective-permute-start.1
  43.7 3.6 collective-permute-start
  47.4 0.6 gather_fusion.4
  48.0 0.6 gather_fusion.3
  48.7 0.6 gather_fusion
  49.3 0.6 gather_fusion.2
  51.1 0.6 fusion.14
  52.0 1.6 collective-permute-done
  53.6 3.2 collective-permute-start.8
  56.8 11.9 %collective-permute-start.7 = (bf16[8,128,64]{1,2,0:T(8,128)(2,1)S(1)}, bf16[8,128,64]{1,2,0:T(8,128)(2,1)S(1)}, u32[]{:S(2)}, u32[]{:S(2)}) collective-permute-start(bf16[8,128,64]{1,2,0:T(8,128)(2,1)S(1)} %fusion.7), channel_id=1, source_target_pairs={{0,432},{8,440},{16,448},{24,456},{32,464},{40,472},{48,480},{56,4... | collective-permute-start | bytes 393224 | tf_op jit(solution)/shard_map/ppermute | solution.py:9
  68.9 2.1 collective-permute-start.6
  71.1 10.7 %collective-permute-start.5 = (bf16[8,128,64]{1,2,0:T(8,128)(2,1)S(1)}, bf16[8,128,64]{1,2,0:T(8,128)(2,1)S(1)}, u32[]{:S(2)}, u32[]{:S(2)}) collective-permute-start(bf16[8,128,64]{1,2,0:T(8,128)(2,1)S(1)} %fusion.6), channel_id=1, source_target_pairs={{0,328},{8,336},{16,344},{24,352},{32,360},{40,368},{48,376},{56,3... | collective-permute-start | bytes 393224 | tf_op jit(solution)/shard_map/ppermute | solution.py:9
  82.0 4.7 %collective-permute-start.4 = (s32[8]{0:T(128)S(1)}, s32[8]{0:T(128)S(1)}, u32[]{:S(2)}, u32[]{:S(2)}) collective-permute-start(s32[8]{0:T(128)S(1)} %get-tuple-element.30), channel_id=1, source_target_pairs={{0,328},{8,336},{16,344},{24,352},{32,360},{40,368},{48,376},{56,3... | collective-permute-start | bytes 104 | tf_op jit(solution)/shard_map/ppermute | solution.py:9
  86.7 5.0 %collective-permute-start.3 = (bf16[8,128,64]{1,2,0:T(8,128)(2,1)S(1)}, bf16[8,128,64]{1,2,0:T(8,128)(2,1)S(1)}, u32[]{:S(2)}, u32[]{:S(2)}) collective-permute-start(bf16[8,128,64]{1,2,0:T(8,128)(2,1)S(1)} %fusion.5), channel_id=1, source_target_pairs={{0,216},{8,224},{16,232},{24,240},{32,248},{40,256},{48,264},{56,2... | collective-permute-start | bytes 393224 | tf_op jit(solution)/shard_map/ppermute | solution.py:9
  91.9 7.5 %collective-permute-start.2 = (s32[8]{0:T(128)S(1)}, s32[8]{0:T(128)S(1)}, u32[]{:S(2)}, u32[]{:S(2)}) collective-permute-start(s32[8]{0:T(128)S(1)} %get-tuple-element.28), channel_id=1, source_target_pairs={{0,216},{8,224},{16,232},{24,240},{32,248},{40,256},{48,264},{56,2... | collective-permute-start | bytes 104 | tf_op jit(solution)/shard_map/ppermute | solution.py:9
  99.8 3.7 collective-permute-done.2
  103.8 1.8 fusion.60
  106.3 0.6 slice_bitcast_fusion
  106.9 41.2 %reduce-scatter.2.cloned.1.call-done = f32[64,1024]{1,0:T(8,128)} async-done(((f32[512,1024]{1,0:T(8,128)}), f32[64,1024]{1,0:T(8,128)}) %reduce-scatter.2.cloned.1.call-update) | async-done | bytes 262160 | tf_op jit(solution)/shard_map/reduce_scatter | solution.py:80
  148.1 1.8 fusion.24
  150.1 0.6 compare_and_fusion
  150.7 32.4 %all-gather.2.cloned.1.call-done = bf16[1024,512]{0,1:T(8,128)(2,1)} async-done(((bf16[1024,64]{0,1:T(8,128)(2,1)}), bf16[1024,512]{0,1:T(8,128)(2,1)}) %all-gather.2.cloned.1.call-update) | async-done | bytes 1048592 | tf_op jit(solution)/shard_map/all_gather | solution.py:94
  183.1 1.5 fusion.145
  184.6 0.6 gather_fusion.7
  185.2 0.6 gather_fusion.8
  185.8 0.7 broadcast_select_fusion.5
  186.5 9.3 %collective-permute-start.12 = (bf16[8,128,64]{1,2,0:T(8,128)(2,1)}, bf16[8,128,64]{1,2,0:T(8,128)(2,1)}, u32[]{:S(2)}, u32[]{:S(2)}) collective-permute-start(bf16[8,128,64]{1,2,0:T(8,128)(2,1)} %broadcast_select_fusion.5), channel_id=1, source_target_pairs={{0,664},{8,672},{16,680},{24,688},{32,696},{40,704},{48,712},{56,7... | collective-permute-start | bytes 393224 | tf_op jit(solution)/shard_map/ppermute | solution.py:9
  195.8 0.6 gather_fusion.9
  196.4 0.7 broadcast_select_fusion.4
  197.2 6.1 %collective-permute-start.13 = (bf16[8,128,64]{1,2,0:T(8,128)(2,1)}, bf16[8,128,64]{1,2,0:T(8,128)(2,1)}, u32[]{:S(2)}, u32[]{:S(2)}) collective-permute-start(bf16[8,128,64]{1,2,0:T(8,128)(2,1)} %broadcast_select_fusion.4), channel_id=1, source_target_pairs={{0,552},{8,560},{16,568},{24,576},{32,584},{40,592},{48,600},{56,6... | collective-permute-start | bytes 393224 | tf_op jit(solution)/shard_map/ppermute | solution.py:9
  203.2 0.6 gather_fusion.10
  203.8 0.7 broadcast_select_fusion.3
  204.6 3.9 collective-permute-start.14
  208.5 0.6 gather_fusion.11
  209.1 0.8 broadcast_select_fusion.2
  209.8 9.6 %collective-permute-start.15 = (bf16[8,128,64]{1,2,0:T(8,128)(2,1)}, bf16[8,128,64]{1,2,0:T(8,128)(2,1)}, u32[]{:S(2)}, u32[]{:S(2)}) collective-permute-start(bf16[8,128,64]{1,2,0:T(8,128)(2,1)} %broadcast_select_fusion.2), channel_id=1, source_target_pairs={{0,336},{8,344},{16,352},{24,360},{32,368},{40,376},{48,384},{56,3... | collective-permute-start | bytes 393224 | tf_op jit(solution)/shard_map/ppermute | solution.py:9
  219.5 0.6 gather_fusion.12
  220.0 0.7 broadcast_select_fusion.1
  220.8 2.0 collective-permute-start.16
  223.4 1.2 fusion.59
  224.6 1.0 convolution_bitcast_fusion
  225.7 0.6 fusion.12
  226.4 4.2 collective-permute-start.17
  230.6 1.1 convolution_bitcast_fusion.7
  232.2 1.1 convolution_bitcast_fusion.6
  233.7 1.1 convolution_bitcast_fusion.5
  235.2 1.1 convolution_bitcast_fusion.4
  236.7 1.0 collective-permute-done.16
  238.3 10.2 %collective-permute-done.17 = bf16[8,128,64]{1,2,0:T(8,128)(2,1)S(1)} collective-permute-done((bf16[8,128,64]{1,2,0:T(8,128)(2,1)S(1)}, bf16[8,128,64]{1,2,0:T(8,128)(2,1)S(1)}, u32[]{:S(2)}, u32[]{:S(2)}) %collective-permute-start.17) | collective-permute-done | bytes 131104 | tf_op jit(solution)/shard_map/ppermute | solution.py:9
  249.0 0.8 bitcast_add_fusion
  249.8 191.3 %all-reduce.2.cloned.1.call-done = f32[128,512]{1,0:T(8,128)} async-done(((f32[128,512]{1,0:T(8,128)}), f32[128,512]{1,0:T(8,128)}) %all-reduce.2.cloned.1.call-update) | async-done | bytes 262160 | tf_op jit(solution)/shard_map/psum | solution.py:100
  441.1 1.7 fusion.144
  (102 shorter events, 7.2 us)
Async XLA Ops:
  7.2 43.4 %copy-start = (bf16[1,16,128,128]{3,2,1,0:T(8,128)(2,1)S(1)}, bf16[1,16,128,128]{3,2,1,0:T(8,128)(2,1)}, u32[]{:S(2)}) copy-start(bf16[1,16,128,128]{3,2,1,0:T(8,128)(2,1)} %param.19) | copy-start | bytes 1572868
  7.2 26.9 %copy-start.2 = (bf16[1,6,8,128,128]{4,3,2,1,0:T(8,128)(2,1)S(1)}, bf16[1,6,8,128,128]{4,3,2,1,0:T(8,128)(2,1)}, u32[]{:S(2)}) copy-start(bf16[1,6,8,128,128]{4,3,2,1,0:T(8,128)(2,1)} %param.22) | copy-start | bytes 4718596
  7.2 140.9 %reduce-scatter.2.cloned.1.call-start = ((), (), s32[]{:S(2)}) async-start(), calls=%async_computation.1 | async-start | bytes 2359296 | tf_op jit(solution)/shard_map/reduce_scatter | solution.py:80
  9.1 38.3 %copy-start.14 = (s32[1,16]{1,0:T(1,128)S(1)}, s32[1,16]{1,0:T(1,128)}, u32[]{:S(2)}) copy-start(s32[1,16]{1,0:T(1,128)} %param.21) | copy-start | bytes 196
  10.9 60.1 %collective-permute-start.11 = (bf16[8,128,64]{1,2,0:T(8,128)(2,1)S(1)}, bf16[8,128,64]{1,2,0:T(8,128)(2,1)S(1)}, u32[]{:S(2)}, u32[]{:S(2)}) collective-permute-start(bf16[8,128,64]{1,2,0:T(8,128)(2,1)S(1)} %fusion.9), channel_id=1, source_target_pairs={{0,656},{8,664},{16,672},{24,680},{32,688},{40,696},{48,704},{56,7... | collective-permute-start | bytes 393224 | tf_op jit(solution)/shard_map/ppermute | solution.py:9
  30.5 38.4 %collective-permute-start.10 = (s32[8]{0:T(128)S(1)}, s32[8]{0:T(128)S(1)}, u32[]{:S(2)}, u32[]{:S(2)}) collective-permute-start(s32[8]{0:T(128)S(1)} %get-tuple-element.32), channel_id=1, source_target_pairs={{0,656},{8,664},{16,672},{24,680},{32,688},{40,696},{48,704},{56,7... | collective-permute-start | bytes 104 | tf_op jit(solution)/shard_map/ppermute | solution.py:9
  33.5 15.1 %copy-start.13 = (s32[1,16]{1,0:T(1,128)S(1)}, s32[1,16]{1,0:T(1,128)}, u32[]{:S(2)}) copy-start(s32[1,16]{1,0:T(1,128)} %param.20) | copy-start | bytes 196
  35.1 51.6 %collective-permute-start.9 = (bf16[8,128,64]{1,2,0:T(8,128)(2,1)}, bf16[8,128,64]{1,2,0:T(8,128)(2,1)S(1)}, u32[]{:S(2)}, u32[]{:S(2)}) collective-permute-start(bf16[8,128,64]{1,2,0:T(8,128)(2,1)} %fusion.8), channel_id=1, source_target_pairs={{0,544},{8,552},{16,560},{24,568},{32,576},{40,584},{48,592},{56,6... | collective-permute-start | bytes 393224 | tf_op jit(solution)/shard_map/ppermute | solution.py:9
  38.9 10.9 %copy-start.9 = (s32[1024]{0:T(1024)S(1)}, s32[1024]{0:T(1024)}, u32[]{:S(2)}) copy-start(s32[1024]{0:T(1024)} %param.18) | copy-start | bytes 12292
  39.9 16.9 %collective-permute-start.1 = (bf16[8,128,64]{1,2,0:T(8,128)(2,1)}, bf16[8,128,64]{1,2,0:T(8,128)(2,1)S(1)}, u32[]{:S(2)}, u32[]{:S(2)}) collective-permute-start(bf16[8,128,64]{1,2,0:T(8,128)(2,1)} %fusion.4), channel_id=1, source_target_pairs={{0,104},{8,112},{16,120},{24,128},{32,136},{40,144},{48,152},{56,1... | collective-permute-start | bytes 393224 | tf_op jit(solution)/shard_map/ppermute | solution.py:9
  43.7 9.8 %collective-permute-start = (s32[8]{0:T(128)S(1)}, s32[8]{0:T(128)S(1)}, u32[]{:S(2)}, u32[]{:S(2)}) collective-permute-start(s32[8]{0:T(128)S(1)} %get-tuple-element.31), channel_id=1, source_target_pairs={{0,104},{8,112},{16,120},{24,128},{32,136},{40,144},{48,152},{56,1... | collective-permute-start | bytes 104 | tf_op jit(solution)/shard_map/ppermute | solution.py:9
  50.2 1.8 copy-start.6
  50.2 1.8 copy-start.7
  53.6 28.4 %collective-permute-start.8 = (s32[8]{0:T(128)S(1)}, s32[8]{0:T(128)S(1)}, u32[]{:S(2)}, u32[]{:S(2)}) collective-permute-start(s32[8]{0:T(128)S(1)} %get-tuple-element.33), channel_id=1, source_target_pairs={{0,544},{8,552},{16,560},{24,568},{32,576},{40,584},{48,592},{56,6... | collective-permute-start | bytes 104 | tf_op jit(solution)/shard_map/ppermute | solution.py:9
  56.8 42.6 %collective-permute-start.7 = (bf16[8,128,64]{1,2,0:T(8,128)(2,1)S(1)}, bf16[8,128,64]{1,2,0:T(8,128)(2,1)S(1)}, u32[]{:S(2)}, u32[]{:S(2)}) collective-permute-start(bf16[8,128,64]{1,2,0:T(8,128)(2,1)S(1)} %fusion.7), channel_id=1, source_target_pairs={{0,432},{8,440},{16,448},{24,456},{32,464},{40,472},{48,480},{56,4... | collective-permute-start | bytes 393224 | tf_op jit(solution)/shard_map/ppermute | solution.py:9
  68.9 22.9 %collective-permute-start.6 = (s32[8]{0:T(128)S(1)}, s32[8]{0:T(128)S(1)}, u32[]{:S(2)}, u32[]{:S(2)}) collective-permute-start(s32[8]{0:T(128)S(1)} %get-tuple-element.29), channel_id=1, source_target_pairs={{0,432},{8,440},{16,448},{24,456},{32,464},{40,472},{48,480},{56,4... | collective-permute-start | bytes 104 | tf_op jit(solution)/shard_map/ppermute | solution.py:9
  71.1 28.6 %collective-permute-start.5 = (bf16[8,128,64]{1,2,0:T(8,128)(2,1)S(1)}, bf16[8,128,64]{1,2,0:T(8,128)(2,1)S(1)}, u32[]{:S(2)}, u32[]{:S(2)}) collective-permute-start(bf16[8,128,64]{1,2,0:T(8,128)(2,1)S(1)} %fusion.6), channel_id=1, source_target_pairs={{0,328},{8,336},{16,344},{24,352},{32,360},{40,368},{48,376},{56,3... | collective-permute-start | bytes 393224 | tf_op jit(solution)/shard_map/ppermute | solution.py:9
  82.0 21.9 %copy-start.4 = (bf16[1024,64]{0,1:T(8,128)(2,1)S(1)}, bf16[1024,64]{0,1:T(8,128)(2,1)}, u32[]{:S(2)}) copy-start(bf16[1024,64]{0,1:T(8,128)(2,1)} %param.15) | copy-start | bytes 393220
  82.0 17.6 %collective-permute-start.4 = (s32[8]{0:T(128)S(1)}, s32[8]{0:T(128)S(1)}, u32[]{:S(2)}, u32[]{:S(2)}) collective-permute-start(s32[8]{0:T(128)S(1)} %get-tuple-element.30), channel_id=1, source_target_pairs={{0,328},{8,336},{16,344},{24,352},{32,360},{40,368},{48,376},{56,3... | collective-permute-start | bytes 104 | tf_op jit(solution)/shard_map/ppermute | solution.py:9
  86.7 16.9 %collective-permute-start.3 = (bf16[8,128,64]{1,2,0:T(8,128)(2,1)S(1)}, bf16[8,128,64]{1,2,0:T(8,128)(2,1)S(1)}, u32[]{:S(2)}, u32[]{:S(2)}) collective-permute-start(bf16[8,128,64]{1,2,0:T(8,128)(2,1)S(1)} %fusion.5), channel_id=1, source_target_pairs={{0,216},{8,224},{16,232},{24,240},{32,248},{40,256},{48,264},{56,2... | collective-permute-start | bytes 393224 | tf_op jit(solution)/shard_map/ppermute | solution.py:9
  91.9 11.7 %collective-permute-start.2 = (s32[8]{0:T(128)S(1)}, s32[8]{0:T(128)S(1)}, u32[]{:S(2)}, u32[]{:S(2)}) collective-permute-start(s32[8]{0:T(128)S(1)} %get-tuple-element.28), channel_id=1, source_target_pairs={{0,216},{8,224},{16,232},{24,240},{32,248},{40,256},{48,264},{56,2... | collective-permute-start | bytes 104 | tf_op jit(solution)/shard_map/ppermute | solution.py:9
  105.6 0.7 copy-start.8
  105.6 42.5 %copy-start.5 = (bf16[1024,64]{0,1:T(8,128)(2,1)S(1)}, bf16[1024,64]{0,1:T(8,128)(2,1)}, u32[]{:S(2)}) copy-start(bf16[1024,64]{0,1:T(8,128)(2,1)} %param.25) | copy-start | bytes 393220
  105.7 77.4 %all-gather.2.cloned.1.call-start = ((), (), s32[]{:S(2)}) async-start(), calls=%async_computation.2 | async-start | bytes 1179648 | tf_op jit(solution)/shard_map/all_gather | solution.py:94
  149.9 291.2 %all-reduce.2.cloned.1.call-start = ((), (), s32[]{:S(2)}) async-start(), calls=%async_computation.3 | async-start | bytes 524288 | tf_op jit(solution)/shard_map/psum | solution.py:100
  186.5 39.9 %collective-permute-start.12 = (bf16[8,128,64]{1,2,0:T(8,128)(2,1)}, bf16[8,128,64]{1,2,0:T(8,128)(2,1)}, u32[]{:S(2)}, u32[]{:S(2)}) collective-permute-start(bf16[8,128,64]{1,2,0:T(8,128)(2,1)} %broadcast_select_fusion.5), channel_id=1, source_target_pairs={{0,664},{8,672},{16,680},{24,688},{32,696},{40,704},{48,712},{56,7... | collective-permute-start | bytes 393224 | tf_op jit(solution)/shard_map/ppermute | solution.py:9
  196.4 27.0 %copy-start.1 = (bf16[1024,512]{0,1:T(8,128)(2,1)S(1)}, bf16[1024,512]{0,1:T(8,128)(2,1)}, u32[]{:S(2)}) copy-start(bf16[1024,512]{0,1:T(8,128)(2,1)} %all-gather.2.cloned.1.call-done) | copy-start | bytes 3145732
  197.2 35.0 %collective-permute-start.13 = (bf16[8,128,64]{1,2,0:T(8,128)(2,1)}, bf16[8,128,64]{1,2,0:T(8,128)(2,1)}, u32[]{:S(2)}, u32[]{:S(2)}) collective-permute-start(bf16[8,128,64]{1,2,0:T(8,128)(2,1)} %broadcast_select_fusion.4), channel_id=1, source_target_pairs={{0,552},{8,560},{16,568},{24,576},{32,584},{40,592},{48,600},{56,6... | collective-permute-start | bytes 393224 | tf_op jit(solution)/shard_map/ppermute | solution.py:9
  204.6 29.1 %collective-permute-start.14 = (bf16[8,128,64]{1,2,0:T(8,128)(2,1)}, bf16[8,128,64]{1,2,0:T(8,128)(2,1)}, u32[]{:S(2)}, u32[]{:S(2)}) collective-permute-start(bf16[8,128,64]{1,2,0:T(8,128)(2,1)} %broadcast_select_fusion.3), channel_id=1, source_target_pairs={{0,440},{8,448},{16,456},{24,464},{32,472},{40,480},{48,488},{56,4... | collective-permute-start | bytes 393224 | tf_op jit(solution)/shard_map/ppermute | solution.py:9
  209.8 25.4 %collective-permute-start.15 = (bf16[8,128,64]{1,2,0:T(8,128)(2,1)}, bf16[8,128,64]{1,2,0:T(8,128)(2,1)}, u32[]{:S(2)}, u32[]{:S(2)}) collective-permute-start(bf16[8,128,64]{1,2,0:T(8,128)(2,1)} %broadcast_select_fusion.2), channel_id=1, source_target_pairs={{0,336},{8,344},{16,352},{24,360},{32,368},{40,376},{48,384},{56,3... | collective-permute-start | bytes 393224 | tf_op jit(solution)/shard_map/ppermute | solution.py:9
  220.8 16.9 %collective-permute-start.16 = (bf16[8,128,64]{1,2,0:T(8,128)(2,1)}, bf16[8,128,64]{1,2,0:T(8,128)(2,1)S(1)}, u32[]{:S(2)}, u32[]{:S(2)}) collective-permute-start(bf16[8,128,64]{1,2,0:T(8,128)(2,1)} %broadcast_select_fusion.1), channel_id=1, source_target_pairs={{0,224},{8,232},{16,240},{24,248},{32,256},{40,264},{48,272},{56,2... | collective-permute-start | bytes 393224 | tf_op jit(solution)/shard_map/ppermute | solution.py:9
  223.4 2.3 copy-start.15
  224.6 1.7 copy-start.12
  224.6 6.0 %copy-start.3 = (bf16[1,6,8,128,128]{4,3,2,1,0:T(8,128)(2,1)S(1)}, bf16[1,6,8,128,128]{4,3,2,1,0:T(8,128)(2,1)}, u32[]{:S(2)}) copy-start(bf16[1,6,8,128,128]{4,3,2,1,0:T(8,128)(2,1)} %param.22) | copy-start | bytes 4718596
  224.6 7.1 %copy-start.11 = (s32[8]{0:T(128)S(1)}, s32[8]{0:T(128)}, u32[]{:S(2)}) copy-start(s32[8]{0:T(128)} %get-tuple-element.26) | copy-start | bytes 100
  225.7 7.6 %copy-start.10 = (s32[8]{0:T(128)S(1)}, s32[8]{0:T(128)}, u32[]{:S(2)}) copy-start(s32[8]{0:T(128)} %get-tuple-element.25) | copy-start | bytes 100
  226.4 22.0 %collective-permute-start.17 = (bf16[8,128,64]{1,2,0:T(8,128)(2,1)S(1)}, bf16[8,128,64]{1,2,0:T(8,128)(2,1)S(1)}, u32[]{:S(2)}, u32[]{:S(2)}) collective-permute-start(bf16[8,128,64]{1,2,0:T(8,128)(2,1)S(1)} %broadcast_select_fusion), channel_id=1, source_target_pairs={{0,112},{8,120},{16,128},{24,136},{32,144},{40,152},{48,160},{56,1... | collective-permute-start | bytes 393224 | tf_op jit(solution)/shard_map/ppermute | solution.py:9
Sparse Core Ops, SparseCore 0:
  105.8 42.2 reduce-scatter.1
  151.1 31.8 all-gather.1
  224.7 216.2 all-reduce.1
where the time goes:
time: 456 us; the launch traced here: 449 us
  waiting for transfers between devices  281 us (62%)
  starting transfers between devices  113 us (25%)
  matrix products  19.8 us (4%)
  between operations  14.6 us (3%)
  local copies, waits for them, and re-layouts  12.3 us (3%)
  other arithmetic  8.4 us (2%)
    psum x1, waiting for transfers between devices, body(): grad_all = lax.psum(grad_local, 'dom')  191 us
    ppermute x18, starting transfers between devices, shifted(): lax.ppermute(x, axis, [(i, (i + by) % devices) for i in range(devices)])  113 us
    reduce_scatter x1, waiting for transfers between devices, body(): lax.psum_scatter(lax.dot_general(weights, stacked, (((0,), (1,)), ((), ()...  41.2 us
    all_gather x1, waiting for transfers between devices, body(): lax.all_gather(dpre, 'feat', axis=1, tiled=True)  32.4 us
    ppermute x18, waiting for transfers between devices, shifted(): lax.ppermute(x, axis, [(i, (i + by) % devices) for i in range(devices)])  16.4 us
  transfers between devices with their start and end apart: 21, of which 7 were waited for; matrix products, arithmetic and copies ran while one was open for 6% of the time, Pallas kernels for 0%

commit v1 on v0

v1 whole, which is shorter than its diff:
```python
import functools

import jax
import jax.numpy as jnp
from jax import lax
from jax.experimental import pallas as pl
from jax.experimental.pallas import tpu as pltpu
from jax.sharding import PartitionSpec as P

Z_CHIPS = 12
CORES = 2
MESH = pl.DeviceIdType.MESH
F32 = jnp.float32
BF16 = jnp.bfloat16


def kernel(
    nd,
    nf,
    offsets,
    ld,
    ls,
    rd,
    rs,
    xt,
    ct,
    ws,
    wn,
    deg,
    lv,
    rv,
    out,
    gx,
    gs,
    gn,
    xb,
    accs,
    loc,
    parts,
    psend,
    precv,
    wt,
    wrecv,
    wsn,
    xfull,
    afull,
    dfull,
    dsb,
    dr0,
    dr1,
    dr2,
    dr3,
    dr4,
    dr5,
    gsend,
    gyrecv,
    gz,
    gfin,
    pre,
    fs,
    fr,
    bs,
    br,
    wss,
    wsr,
    xs,
    xr,
    as_,
    ar,
    ds,
    dr,
    gys,
    gyr,
    gzs,
    gzr,
    gas,
    gar,
):
    width, rows = xt.shape
    nb = xb.shape[0]
    blk = xb.shape[2]
    drecv = [dr0, dr1, dr2, dr3, dr4, dr5]
    per = rv.shape[1]
    nz = Z_CHIPS
    ny = nd // nz
    nx = nf // CORES
    o = offsets
    me = lax.axis_index("dom")
    f = lax.axis_index("feat")
    y, z = me // nz, me % nz
    x, c = f // CORES, f % CORES
    f_sib = x * CORES + (CORES - 1 - c)
    f_left = ((x + nx - 1) % nx) * CORES + c
    f_right = ((x + 1) % nx) * CORES + c
    f_opp = ((x + 2) % nx) * CORES + c

    def dom_at(by):
        return (me + by + nd) % nd

    up = [o[2] - o[1], o[1] - o[0], o[0]]
    down = [o[4] - o[3], o[5] - o[4], nd - o[5]]

    barrier = pltpu.get_barrier_semaphore()
    near = sorted({h % nd for h in up + down} | {(nd - h) % nd for h in up + down})
    partners = [(dom_at(h), f) for h in near]
    partners += [(me, (f + k) % nf) for k in range(1, nf)]
    partners += [(y * nz + (z + k) % nz, f) for k in range(1, nz)]
    partners += [(((y + k) % ny) * nz + z, f) for k in range(1, ny)]
    for partner in partners:
        pl.semaphore_signal(barrier, inc=1, device_id=partner, device_id_type=MESH)

    def push(src, dst, send, recv, dom, feat):
        copy = pltpu.make_async_remote_copy(
            src_ref=src,
            dst_ref=dst,
            send_sem=send,
            recv_sem=recv,
            device_id=(dom, feat),
            device_id_type=MESH,
        )
        copy.start()
        return copy

    def collect(vals, first, pick, put, blocks, dims, acc):
        for t in range(per):
            parts[t] = lax.dot_general(
                blocks[pick[t]], vals[first + t], dims, preferred_element_type=F32
            )
        for b in range(nb):
            total = jnp.zeros((width, blk), F32)
            for t in range(per):
                total = total + jnp.where(put[t] == b, parts[t], 0.0)
            acc(b, total)

    def remote_forward(r, acc):
        collect(
            rv.at[r],
            0,
            [rs[r, t] for t in range(per)],
            [rd[r, t] for t in range(per)],
            xb,
            (((1,), (1,)), ((), ())),
            acc,
        )

    def to_send(k):
        def put(b, total):
            psend[k, b] = total.astype(BF16)

        return put

    def to_acc(k):
        def put(b, total):
            accs[k, b] = total

        return put

    for b in range(nb):
        xb[b] = xt[:, b * blk : (b + 1) * blk]
    remote_forward(2, to_send(0))
    remote_forward(3, to_send(1))
    pl.semaphore_wait(barrier, len(partners))

    fwd = [None] * 6
    fwd[0] = push(psend.at[0], precv.at[0], fs.at[0], fr.at[0], dom_at(up[0]), f)
    fwd[1] = push(psend.at[1], precv.at[1], fs.at[1], fr.at[1], dom_at(-down[0]), f)

    xfull[f] = xt[...]
    early = []
    for k in range(1, nf):
        to = (f + k) % nf
        early.append(push(xt, xfull.at[f], xs.at[k], xr.at[k], me, to))
    for q in range(ws.shape[1] // blk):
        cols = jnp.concatenate(
            [ws[:, q * blk : (q + 1) * blk], wn[:, q * blk : (q + 1) * blk]], axis=0
        )
        turned = cols.T
        for h in range(blk // width):
            wt[q * (blk // width) + h] = turned[h * width : (h + 1) * width]
    wrecv[f] = wt[f]
    for k in range(1, nf):
        to = (f + k) % nf
        early.append(push(wt.at[to], wrecv.at[f], wss.at[k], wsr.at[k], me, to))

    remote_forward(1, to_acc(0))
    remote_forward(4, to_acc(1))
    for side, hop in ((0, up[1]), (1, -down[1])):
        fwd[side].wait_recv()
        psend[2 + side] = (accs[side] + precv[side].astype(F32)).astype(BF16)
        k = 2 + side
        fwd[k] = push(psend.at[k], precv.at[k], fs.at[k], fr.at[k], dom_at(hop), f)
    remote_forward(0, to_acc(0))
    remote_forward(5, to_acc(1))
    for side, hop in ((0, up[2]), (1, -down[2])):
        fwd[2 + side].wait_recv()
        k = 4 + side
        psend[k] = (accs[side] + precv[2 + side].astype(F32)).astype(BF16)
        fwd[k] = push(psend.at[k], precv.at[k], fs.at[k], fr.at[k], dom_at(hop), f)

    def to_loc(b, total):
        loc[b] = total

    def add_loc(b, total):
        loc[b] = loc[b] + total

    for g in range(lv.shape[0] // per):
        collect(
            lv,
            g * per,
            [ls[0, g * per + t] for t in range(per)],
            [ld[0, g * per + t] for t in range(per)],
            xb,
            (((1,), (1,)), ((), ())),
            add_loc if g else to_loc,
        )
    for copy in early:
        copy.wait_recv()
    pair = blk // width
    for half, dst in ((0, 0), (1, 1)):
        for q in range(nf // pair):
            wsn[dst, :, q * blk : (q + 1) * blk] = jnp.concatenate(
                [wrecv[q * pair + h][:, half * width : (half + 1) * width] for h in range(pair)],
                axis=1,
            )
    pre[...] = jnp.dot(
        wsn[0], xfull[...].reshape(nf * width, rows), preferred_element_type=F32
    )
    inverse = 1.0 / deg[...].astype(F32)
    fwd[4].wait_recv()
    fwd[5].wait_recv()
    for b in range(nb):
        sums = loc[b] + precv[4, b].astype(F32) + precv[5, b].astype(F32)
        afull[f, :, b * blk : (b + 1) * blk] = (
            sums * inverse[:, b * blk : (b + 1) * blk]
        ).astype(BF16)

    half = width // 2

    def gather(full, send, recv):
        def go(k, which, feat, low=0, size=width):
            part = full.at[which, pl.ds(low, size)]
            return push(part, part, send.at[k], recv.at[k], me, feat)

        if nx == 1:
            copy = go(0, f, f_sib)
            copy.wait()
            return
        sent = [go(1, f, f_right), go(2, f, f_left), go(0, f, f_sib)]
        sent[0].wait_recv()
        sent.append(go(4, f_left, f_right, 0, half))
        sent.append(go(3, f_left, f_sib))
        sent[1].wait_recv()
        sent.append(go(6, f_right, f_left, half, half))
        sent.append(go(5, f_right, f_sib))
        sent[3].wait_recv()
        sent.append(go(7, f_opp, f_sib, 0, half))
        sent[5].wait_recv()
        sent.append(go(8, f_opp, f_sib, half, half))
        for k in (2, 4, 6, 7, 8):
            sent[k].wait_recv()
        for copy in sent:
            copy.wait_send()

    gather(afull, as_, ar)
    total = pre[...] + jnp.dot(
        wsn[1], afull[...].reshape(nf * width, rows), preferred_element_type=F32
    )
    sigma = 1.0 / (1.0 + jnp.exp(-total))
    out[...] = (total * sigma).astype(BF16)
    dfull[f] = (ct[...].astype(F32) * sigma * (1.0 + total * (1.0 - sigma))).astype(BF16)

    gather(dfull, ds, dr)
    dall = dfull[...].reshape(nf * width, rows)
    dagg = jnp.dot(wn[...], dall, preferred_element_type=F32)
    for b in range(nb):
        dsb[b] = (
            dagg[:, b * blk : (b + 1) * blk] * inverse[:, b * blk : (b + 1) * blk]
        ).astype(BF16)

    back = [None] * 6
    back_down = [o[0], o[1] - o[0], o[2] - o[1]]
    back_up = [nd - o[5], o[5] - o[4], o[4] - o[3]]
    back[0] = push(dsb, drecv[0], bs.at[0], br.at[0], dom_at(-back_down[0]), f)
    back[1] = push(dsb, drecv[1], bs.at[1], br.at[1], dom_at(back_up[0]), f)

    gx[...] = jnp.dot(ws[...], dall, preferred_element_type=F32)
    grad = lax.dot_general(
        jnp.concatenate([xt[...], afull[f]], axis=0),
        dall,
        (((1,), (1,)), ((), ())),
        preferred_element_type=F32,
    )
    slab = gsend.shape[1]
    for k in range(ny):
        gsend[k] = grad[k * slab : (k + 1) * slab].astype(BF16)
    gyrecv[y] = gsend[y]
    gy_copies = []
    for k in range(1, ny):
        to = (y + k) % ny
        gy_copies.append(
            push(gsend.at[to], gyrecv.at[y], gys.at[k], gyr.at[k], to * nz + z, f)
        )

    def add_gx(b, total):
        gx[:, b * blk : (b + 1) * blk] = gx[:, b * blk : (b + 1) * blk] + total

    nn = (((1,), (0,)), ((), ()))
    for g in range(lv.shape[0] // per):
        collect(
            lv,
            g * per,
            [ld[0, g * per + t] for t in range(per)],
            [ls[0, g * per + t] for t in range(per)],
            dsb,
            nn,
            add_gx,
        )

    def remote_back(r, k):
        collect(
            rv.at[r],
            0,
            [rd[r, t] for t in range(per)],
            [rs[r, t] for t in range(per)],
            drecv[k],
            nn,
            add_gx,
        )

    def relay(k, hop):
        back[k].wait_recv()
        if k < 4:
            n = k + 2
            back[n] = push(drecv[k], drecv[n], bs.at[n], br.at[n], dom_at(hop), f)

    relay(0, -back_down[1])
    relay(1, back_up[1])
    for copy in gy_copies:
        copy.wait_recv()
    mine = gyrecv[0].astype(F32)
    for k in range(1, ny):
        mine = mine + gyrecv[k].astype(F32)
    gz[z] = mine.astype(BF16)
    gz_copies = []
    for k in range(1, nz):
        to = (z + k) % nz
        gz_copies.append(push(gz.at[z], gz.at[z], gzs.at[k], gzr.at[k], y * nz + to, f))
    remote_back(0, 0)
    remote_back(5, 1)
    relay(2, -back_down[2])
    relay(3, back_up[2])
    for copy in gz_copies:
        copy.wait_recv()
    mine = gz[0].astype(F32)
    for k in range(1, nz):
        mine = mine + gz[k].astype(F32)
    gfin[y] = mine.astype(BF16)
    ga_copies = []
    for k in range(1, ny):
        to = (y + k) % ny
        ga_copies.append(push(gfin.at[y], gfin.at[y], gas.at[k], gar.at[k], to * nz + z, f))
    remote_back(1, 2)
    remote_back(4, 3)
    relay(4, 0)
    remote_back(2, 4)
    relay(5, 0)
    remote_back(3, 5)
    for copy in ga_copies:
        copy.wait_recv()
    result = gfin[...].reshape(2 * width, gfin.shape[2]).astype(F32)
    gs[...] = result[:width]
    gn[...] = result[width:]
    for copy in fwd + early + back + gy_copies + gz_copies + ga_copies:
        copy.wait_send()


def body(
    features,
    w_self,
    w_neigh,
    degree,
    local_vals,
    local_dst,
    local_src,
    remote_vals,
    remote_dst,
    remote_src,
    cotangent,
):
    rows, width = features.shape
    blk = local_vals.shape[-1]
    nb = rows // blk
    rounds, per = remote_vals.shape[1:3]
    wide = w_self.shape[1]
    nd = lax.axis_size("dom")
    nf = lax.axis_size("feat")
    ny = nd // Z_CHIPS
    offsets = [(step + 1) * nd // (rounds + 1) for step in range(rounds)]
    slab = 2 * width // ny
    dma = pltpu.SemaphoreType.DMA
    vmem = pl.BlockSpec(memory_space=pltpu.VMEM)
    smem = pl.BlockSpec(memory_space=pltpu.SMEM)
    blocks = (nb, width, blk)
    out, gx, gs, gn = pl.pallas_call(
        functools.partial(kernel, nd, nf, offsets),
        out_shape=(
            jax.ShapeDtypeStruct((width, rows), BF16),
            jax.ShapeDtypeStruct((width, rows), F32),
            jax.ShapeDtypeStruct((width, wide), F32),
            jax.ShapeDtypeStruct((width, wide), F32),
        ),
        in_specs=[smem] * 4 + [vmem] * 7,
        out_specs=(vmem,) * 4,
        scratch_shapes=[
            pltpu.VMEM(blocks, BF16),
            pltpu.VMEM((2,) + blocks, F32),
            pltpu.VMEM(blocks, F32),
            pltpu.VMEM((per, width, blk), F32),
            pltpu.VMEM((6,) + blocks, BF16),
            pltpu.VMEM((6,) + blocks, BF16),
            pltpu.VMEM((nf, width, 2 * width), BF16),
            pltpu.VMEM((nf, width, 2 * width), BF16),
            pltpu.VMEM((2, width, nf * width), BF16),
            pltpu.VMEM((nf, width, rows), BF16),
            pltpu.VMEM((nf, width, rows), BF16),
            pltpu.VMEM((nf, width, rows), BF16),
            pltpu.VMEM(blocks, BF16),
        ]
        + [pltpu.VMEM(blocks, BF16)] * 6
        + [
            pltpu.VMEM((ny, slab, wide), BF16),
            pltpu.VMEM((ny, slab, wide), BF16),
            pltpu.VMEM((Z_CHIPS, slab, wide), BF16),
            pltpu.VMEM((ny, slab, wide), BF16),
            pltpu.VMEM((width, rows), F32),
            dma((6,)),
            dma((6,)),
            dma((6,)),
            dma((6,)),
            dma((nf,)),
            dma((nf,)),
            dma((nf,)),
            dma((nf,)),
            dma((9,)),
            dma((9,)),
            dma((9,)),
            dma((9,)),
            dma((ny,)),
            dma((ny,)),
            dma((Z_CHIPS,)),
            dma((Z_CHIPS,)),
            dma((ny,)),
            dma((ny,)),
        ],
        compiler_params=pltpu.CompilerParams(
            collective_id=0, has_side_effects=True, vmem_limit_bytes=40 * 1024 * 1024
        ),
    )(
        local_dst,
        local_src,
        remote_dst[0],
        remote_src[0],
        features.T,
        cotangent.T,
        w_self,
        w_neigh,
        degree.reshape(1, rows),
        local_vals[0],
        remote_vals[0],
    )
    return out.T, gx.T, gs, gn


def solution(mesh):
    placed = (
        P("dom", "feat"),
        P("feat", None),
        P("feat", None),
        P("dom"),
        P("dom", None, None, None),
        P("dom", None),
        P("dom", None),
        P("dom", None, None, None, None),
        P("dom", None, None),
        P("dom", None, None),
        P("dom", "feat"),
    )
    return jax.shard_map(
        body,
        mesh=mesh,
        in_specs=placed,
        out_specs=(P("dom", "feat"), P("dom", "feat"), P("feat", None), P("feat", None)),
        check_vma=False,
    )
```

time: 456 us -> 116 us (0.25)
  the two profiles are of different devices: /device:TPU:1 before, /device:TPU:66 now
where the time goes in v1:
time: 116 us; the launch traced here: 115 us
  Pallas kernels  103 us (89%)
  local copies, waits for them, and re-layouts  11.3 us (10%)
    pallas_call x1, Pallas kernels, body(): pl.pallas_call(functools.partial(kernel, nd, nf, offsets), out_shape=(jax...  103 us
    unnamed x23, local copies, waits for them, and re-layouts  11.3 us

profile of v1, /device:TPU:66, one launch (start us, length us, event | category | flops | bytes accessed | tf_op | source)
XLA Modules:
  0.0 115.3 jit_solution(3153573711048633498)
XLA Ops:
  0.6 0.7 copy_bitcast_fusion
  1.3 0.0 copy-start
  1.3 1.4 %copy-done = bf16[1,6,8,128,128]{4,3,2,1,0:T(8,128)(2,1)S(1)} copy-done((bf16[1,6,8,128,128]{4,3,2,1,0:T(8,128)(2,1)S(1)}, bf16[1,6,8,128,128]{4,3,2,1,0:T(8,128)(2,1)}, u32[]{:S(2)}) %copy-start) | copy-done | bytes 1572888
  2.7 0.0 copy-start.1
  2.7 1.0 copy-done.1
  3.8 0.0 copy-start.2
  3.8 0.9 copy-done.2
  4.7 0.0 copy-start.3
  4.7 0.9 copy-done.3
  5.6 0.0 copy-start.4
  5.6 0.8 copy-done.4
  6.4 0.0 copy-start.5
  6.4 0.8 copy-done.5
  7.3 0.0 copy-start.6
  7.3 0.7 copy-done.6
  8.0 0.0 copy-start.7
  8.0 0.7 copy-done.7
  8.6 0.0 copy-start.8
  8.6 0.7 copy-done.8
  9.3 103.4 %shard_map.138 = (bf16[64,1024]{1,0:T(8,128)(2,1)S(1)}, f32[64,1024]{1,0:T(8,128)S(1)}, f32[64,512]{1,0:T(8,128)S(1)}, f32[64,512]{1,0:T(8,128)S(1)}) custom-call(s32[1,16]{1,0:T(1,128)S(1)} %copy-done.7, s32[1,16]{1,0:T(1,128)S(1)} %copy-done.8, s32[6,8]{1,0:T(8,128)S(1)} %get-tuple-element.13.rd, s32[6,8]{1,0:T(8,128)S(1)} %get-tuple-element.12.rs, ...), custom_call_target="tpu_custom_call" | custom-call | tf_op jit(solution)/shard_map/pallas_call | solution.py:404
  112.7 0.7 copy.23
  113.3 0.7 copy.24
  114.0 0.7 copy.25
  114.7 0.7 copy.26
Async XLA Ops:
  1.3 1.4 %copy-start = (bf16[1,6,8,128,128]{4,3,2,1,0:T(8,128)(2,1)S(1)}, bf16[1,6,8,128,128]{4,3,2,1,0:T(8,128)(2,1)}, u32[]{:S(2)}) copy-start(bf16[1,6,8,128,128]{4,3,2,1,0:T(8,128)(2,1)} %param.18) | copy-start | bytes 4718596
  2.7 1.0 copy-start.1
  3.8 0.9 copy-start.2
  4.7 0.9 copy-start.3
  5.6 0.8 copy-start.4
  6.4 0.8 copy-start.5
  7.3 0.7 copy-start.6
  8.0 0.7 copy-start.7
  8.6 0.7 copy-start.8

commit v2 on v1

--- a/solution.py
+++ b/solution.py
@@ -9,73 +9,81 @@
 
 Z_CHIPS = 12
 CORES = 2
+CUTS = 2
 MESH = pl.DeviceIdType.MESH
 F32 = jnp.float32
 BF16 = jnp.bfloat16
 
 
-def kernel(
-    nd,
-    nf,
-    offsets,
-    ld,
-    ls,
-    rd,
-    rs,
-    xt,
-    ct,
-    ws,
-    wn,
-    deg,
-    lv,
-    rv,
-    out,
-    gx,
-    gs,
-    gn,
-    xb,
-    accs,
-    loc,
-    parts,
-    psend,
-    precv,
-    wt,
-    wrecv,
-    wsn,
-    xfull,
-    afull,
-    dfull,
-    dsb,
-    dr0,
-    dr1,
-    dr2,
-    dr3,
-    dr4,
-    dr5,
-    gsend,
-    gyrecv,
-    gz,
-    gfin,
-    pre,
-    fs,
-    fr,
-    bs,
-    br,
-    wss,
-    wsr,
-    xs,
-    xr,
-    as_,
-    ar,
-    ds,
-    dr,
-    gys,
-    gyr,
-    gzs,
-    gzr,
-    gas,
-    gar,
-):
+def kernel(nd, nf, offsets, *refs):
+    ins, refs = refs[:11], refs[11:]
+    (out, gx, gs, gn), refs = refs[:4], refs[4:]
+    held, refs = refs[:11], refs[11:]
+    ld, ls, rd, rs, xt, ct, ws, wn, deg, lv, rv = held
+    (
+        xb,
+        accs,
+        loc,
+        parts,
+        psend,
+        precv,
+        wt,
+        wrecv,
+        wsn,
+        xfull,
+        afull,
+        dfull,
+        dsb,
+        dr0,
+        dr1,
+        dr2,
+        dr3,
+        dr4,
+        dr5,
+        gsend,
+        gyrecv,
+        gz,
+        gfin,
+        pre,
+        load_in,
+        load_rv,
+        fs,
+        fr,
+        bs,
+        br,
+        wss,
+        wsr,
+        xs,
+        xr,
+        as_,
+        ar,
+        ds,
+        dr,
+        gys,
+        gyr,
+        gzs,
+        gzr,
+        gas,
+        gar,
+    ) = refs
+    loads = {}
+    for r in (2, 3):
+        loads["rv", r] = pltpu.make_async_copy(ins[10].at[r], rv.at[r], load_rv.at[r])
+    for i in (2, 3, 4):
+        loads[i] = pltpu.make_async_copy(ins[i], held[i], load_in.at[i])
+    for key in (2, 3, 4, ("rv", 2), ("rv", 3)):
+        loads[key].start()
+    for i in (0, 1, 6, 7, 9, 8, 5):
+        loads[i] = pltpu.make_async_copy(ins[i], held[i], load_in.at[i])
+    for r in (1, 4, 0, 5):
+        loads["rv", r] = pltpu.make_async_copy(ins[10].at[r], rv.at[r], load_rv.at[r])
+    for key in (6, 7, ("rv", 1), ("rv", 4), ("rv", 0), ("rv", 5), 0, 1, 9, 8, 5):
+        loads[key].start()
+
+    def ready(*keys):
+        for key in keys:
+            loads[key].wait()
+
     width, rows = xt.shape
     nb = xb.shape[0]
     blk = xb.shape[2]
@@ -136,8 +144,8 @@
         collect(
             rv.at[r],
             0,
-            [rs[r, t] for t in range(per)],
-            [rd[r, t] for t in range(per)],
+            [rs[r, 0, t] for t in range(per)],
+            [rd[r, 0, t] for t in range(per)],
             xb,
             (((1,), (1,)), ((), ())),
             acc,
@@ -155,21 +163,92 @@
 
         return put
 
+    span = nb // CUTS
+
+    def hop(src, dst, send, recv, k, by):
+        return [
+            push(
+                src.at[pl.ds(j * span, span)],
+                dst.at[pl.ds(j * span, span)],
+                send.at[k, j],
+                recv.at[k, j],
+                dom_at(by),
+                f,
+            )
+            for j in range(CUTS)
+        ]
+
+    quarter = width // 4
+
+    class Ring:
+
+        def __init__(self, full, send, recv):
+            self.full, self.send, self.recv = full, send, recv
+            self.copies, self.used = [], 0
+
+        def go(self, which, feat, low, parts_):
+            part = self.full.at[which, pl.ds(low * quarter, parts_ * quarter)]
+            k = self.used
+            self.used += 1
+            copy = push(part, part, self.send.at[k], self.recv.at[k], me, feat)
+            self.copies.append(copy)
+            return copy
+
+        def start(self):
+            if nx > 1:
+                self.left, self.right = {}, {}
+                for low, high in ((0, 2), (1, 3), (2, 0), (3, 1)):
+                    self.left[low] = self.go(f, f_right, low, 1)
+                    self.right[high] = self.go(f, f_left, high, 1)
+            self.sib = [self.go(f, f_sib, 0, 4)]
+
+        def middle(self):
+            if nx == 1:
+                return
+            self.opp = []
+            for low in (0, 1):
+                self.left[low].wait_recv()
+                self.opp.append((low, self.go(f_left, f_right, low, 1)))
+                self.right[low + 2].wait_recv()
+                self.opp.append((low + 2, self.go(f_right, f_left, low + 2, 1)))
+            self.sib.append(self.go(f_left, f_sib, 0, 2))
+            self.sib.append(self.go(f_right, f_sib, 2, 2))
+            for low in (2, 3):
+                self.left[low].wait_recv()
+                self.right[low - 2].wait_recv()
+            self.sib.append(self.go(f_left, f_sib, 2, 2))
+            self.sib.append(self.go(f_right, f_sib, 0, 2))
+
+        def last(self):
+            if nx == 1:
+                return
+            for low, copy in self.opp:
+                copy.wait_recv()
+                self.sib.append(self.go(f_opp, f_sib, low, 1))
+
+        def finish(self):
+            for copy in self.sib:
+                copy.wait_recv()
+            for copy in self.copies:
+                copy.wait_send()
+
+    ready(2, 3, 4)
     for b in range(nb):
         xb[b] = xt[:, b * blk : (b + 1) * blk]
+    xfull[f] = xt[...]
+    ready(("rv", 2))
     remote_forward(2, to_send(0))
+    ready(("rv", 3))
     remote_forward(3, to_send(1))
     pl.semaphore_wait(barrier, len(partners))
 
     fwd = [None] * 6
-    fwd[0] = push(psend.at[0], precv.at[0], fs.at[0], fr.at[0], dom_at(up[0]), f)
-    fwd[1] = push(psend.at[1], precv.at[1], fs.at[1], fr.at[1], dom_at(-down[0]), f)
-
-    xfull[f] = xt[...]
-    early = []
-    for k in range(1, nf):
-        to = (f + k) % nf
-        early.append(push(xt, xfull.at[f], xs.at[k], xr.at[k], me, to))
+    fwd[0] = hop(psend.at[0], precv.at[0], fs, fr, 0, up[0])
+    fwd[1] = hop(psend.at[1], precv.at[1], fs, fr, 1, -down[0])
+
+    x_ring = Ring(xfull, xs, xr)
+    x_ring.start()
+    ready(6, 7)
     for q in range(ws.shape[1] // blk):
         cols = jnp.concatenate(
             [ws[:, q * blk : (q + 1) * blk], wn[:, q * blk : (q + 1) * blk]], axis=0
@@ -178,24 +257,43 @@
         for h in range(blk // width):
             wt[q * (blk // width) + h] = turned[h * width : (h + 1) * width]
     wrecv[f] = wt[f]
+    early = []
     for k in range(1, nf):
         to = (f + k) % nf
         early.append(push(wt.at[to], wrecv.at[f], wss.at[k], wsr.at[k], me, to))
 
+    ready(("rv", 1), ("rv", 4))
     remote_forward(1, to_acc(0))
     remote_forward(4, to_acc(1))
-    for side, hop in ((0, up[1]), (1, -down[1])):
-        fwd[side].wait_recv()
-        psend[2 + side] = (accs[side] + precv[side].astype(F32)).astype(BF16)
-        k = 2 + side
-        fwd[k] = push(psend.at[k], precv.at[k], fs.at[k], fr.at[k], dom_at(hop), f)
+
+    def add_on(step, ups):
+        for side in (0, 1):
+            fwd[step + side] = []
+        for j in range(CUTS):
+            part = pl.ds(j * span, span)
+            for side in (0, 1):
+                k = step + side
+                fwd[k - 2][j].wait_recv()
+                psend[k, part] = (accs[side, part] + precv[k - 2, part].astype(F32)).astype(BF16)
+                fwd[k].append(
+                    push(
+                        psend.at[k, part],
+                        precv.at[k, part],
+                        fs.at[k, j],
+                        fr.at[k, j],
+                        dom_at(ups[side]),
+                        f,
+                    )
+                )
+
+    add_on(2, (up[1], -down[1]))
+    x_ring.middle()
+    ready(("rv", 0), ("rv", 5))
     remote_forward(0, to_acc(0))
     remote_forward(5, to_acc(1))
-    for side, hop in ((0, up[2]), (1, -down[2])):
-        fwd[2 + side].wait_recv()
-        k = 4 + side
-        psend[k] = (accs[side] + precv[2 + side].astype(F32)).astype(BF16)
-        fwd[k] = push(psend.at[k], precv.at[k], fs.at[k], fr.at[k], dom_at(hop), f)
+    add_on(4, (up[2], -down[2]))
+    x_ring.last()
+    ready(0, 1, 9)
 
     def to_loc(b, total):
         loc[b] = total
@@ -215,6 +313,7 @@
         )
     for copy in early:
         copy.wait_recv()
+    x_ring.finish()
     pair = blk // width
     for half, dst in ((0, 0), (1, 1)):
         for q in range(nf // pair):
@@ -225,41 +324,23 @@
     pre[...] = jnp.dot(
         wsn[0], xfull[...].reshape(nf * width, rows), preferred_element_type=F32
     )
+    ready(8, 5)
     inverse = 1.0 / deg[...].astype(F32)
-    fwd[4].wait_recv()
-    fwd[5].wait_recv()
-    for b in range(nb):
-        sums = loc[b] + precv[4, b].astype(F32) + precv[5, b].astype(F32)
-        afull[f, :, b * blk : (b + 1) * blk] = (
-            sums * inverse[:, b * blk : (b + 1) * blk]
-        ).astype(BF16)
-
-    half = width // 2
+    for j in range(CUTS):
+        fwd[4][j].wait_recv()
+        fwd[5][j].wait_recv()
+        for b in range(j * span, (j + 1) * span):
+            sums = loc[b] + precv[4, b].astype(F32) + precv[5, b].astype(F32)
+            afull[f, :, b * blk : (b + 1) * blk] = (
+                sums * inverse[:, b * blk : (b + 1) * blk]
+            ).astype(BF16)
 
     def gather(full, send, recv):
-        def go(k, which, feat, low=0, size=width):
-            part = full.at[which, pl.ds(low, size)]
-            return push(part, part, send.at[k], recv.at[k], me, feat)
-
-        if nx == 1:
-            copy = go(0, f, f_sib)
-            copy.wait()
-            return
-        sent = [go(1, f, f_right), go(2, f, f_left), go(0, f, f_sib)]
-        sent[0].wait_recv()
-        sent.append(go(4, f_left, f_right, 0, half))
-        sent.append(go(3, f_left, f_sib))
-        sent[1].wait_recv()
-        sent.append(go(6, f_right, f_left, half, half))
-        sent.append(go(5, f_right, f_sib))
-        sent[3].wait_recv()
-        sent.append(go(7, f_opp, f_sib, 0, half))
-        sent[5].wait_recv()
-        sent.append(go(8, f_opp, f_sib, half, half))
-        for k in (2, 4, 6, 7, 8):
-            sent[k].wait_recv()
-        for copy in sent:
-            copy.wait_send()
+        ring = Ring(full, send, recv)
+        ring.start()
+        ring.middle()
+        ring.last()
+        ring.finish()
 
     gather(afull, as_, ar)
     total = pre[...] + jnp.dot(
@@ -271,19 +352,28 @@
 
     gather(dfull, ds, dr)
     dall = dfull[...].reshape(nf * width, rows)
-    dagg = jnp.dot(wn[...], dall, preferred_element_type=F32)
-    for b in range(nb):
-        dsb[b] = (
-            dagg[:, b * blk : (b + 1) * blk] * inverse[:, b * blk : (b + 1) * blk]
-        ).astype(BF16)
-
-    back = [None] * 6
+    back = [[], []] + [None] * 4
     back_down = [o[0], o[1] - o[0], o[2] - o[1]]
     back_up = [nd - o[5], o[5] - o[4], o[4] - o[3]]
-    back[0] = push(dsb, drecv[0], bs.at[0], br.at[0], dom_at(-back_down[0]), f)
-    back[1] = push(dsb, drecv[1], bs.at[1], br.at[1], dom_at(back_up[0]), f)
-
-    gx[...] = jnp.dot(ws[...], dall, preferred_element_type=F32)
+    for j in range(CUTS):
+        low, high = j * span * blk, (j + 1) * span * blk
+        dagg = jnp.dot(wn[...], dall[:, low:high], preferred_element_type=F32)
+        dagg = dagg * inverse[:, low:high]
+        for b in range(span):
+            dsb[j * span + b] = dagg[:, b * blk : (b + 1) * blk].astype(BF16)
+        part = pl.ds(j * span, span)
+        for side, by in ((0, -back_down[0]), (1, back_up[0])):
+            back[side].append(
+                push(
+                    dsb.at[part],
+                    drecv[side].at[part],
+                    bs.at[side, j],
+                    br.at[side, j],
+                    dom_at(by),
+                    f,
+                )
+            )
+
     grad = lax.dot_general(
         jnp.concatenate([xt[...], afull[f]], axis=0),
         dall,
@@ -301,6 +391,8 @@
             push(gsend.at[to], gyrecv.at[y], gys.at[k], gyr.at[k], to * nz + z, f)
         )
 
+    gx[...] = jnp.dot(ws[...], dall, preferred_element_type=F32)
+
     def add_gx(b, total):
         gx[:, b * blk : (b + 1) * blk] = gx[:, b * blk : (b + 1) * blk] + total
 
@@ -320,21 +412,35 @@
         collect(
             rv.at[r],
             0,
-            [rd[r, t] for t in range(per)],
-            [rs[r, t] for t in range(per)],
+            [rd[r, 0, t] for t in range(per)],
+            [rs[r, 0, t] for t in range(per)],
             drecv[k],
             nn,
             add_gx,
         )
 
-    def relay(k, hop):
-        back[k].wait_recv()
-        if k < 4:
-            n = k + 2
-            back[n] = push(drecv[k], drecv[n], bs.at[n], br.at[n], dom_at(hop), f)
-
-    relay(0, -back_down[1])
-    relay(1, back_up[1])
+    def relay(k, by):
+        for j in range(CUTS):
+            part = pl.ds(j * span, span)
+            for side in (0, 1):
+                n = k + 2 + side
+                back[k + side][j].wait_recv()
+                if by is None:
+                    continue
+                if j == 0:
+                    back[n] = []
+                back[n].append(
+                    push(
+                        drecv[k + side].at[part],
+                        drecv[n].at[part],
+                        bs.at[n, j],
+                        br.at[n, j],
+                        dom_at(by[side]),
+                        f,
+                    )
+                )
+
+    relay(0, (-back_down[1], back_up[1]))
     for copy in gy_copies:
         copy.wait_recv()
     mine = gyrecv[0].astype(F32)
@@ -347,8 +453,9 @@
         gz_copies.append(push(gz.at[z], gz.at[z], gzs.at[k], gzr.at[k], y * nz + to, f))
     remote_back(0, 0)
     remote_back(5, 1)
-    relay(2, -back_down[2])
-    relay(3, back_up[2])
+    relay(2, (-back_down[2], back_up[2]))
+    remote_back(1, 2)
+    remote_back(4, 3)
     for copy in gz_copies:
         copy.wait_recv()
     mine = gz[0].astype(F32)
@@ -359,18 +466,15 @@
     for k in range(1, ny):
         to = (y + k) % ny
         ga_copies.append(push(gfin.at[y], gfin.at[y], gas.at[k], gar.at[k], to * nz + z, f))
-    remote_back(1, 2)
-    remote_back(4, 3)
-    relay(4, 0)
+    relay(4, None)
     remote_back(2, 4)
-    relay(5, 0)
     remote_back(3, 5)
     for copy in ga_copies:
         copy.wait_recv()
     result = gfin[...].reshape(2 * width, gfin.shape[2]).astype(F32)
     gs[...] = result[:width]
     gn[...] = result[width:]
-    for copy in fwd + early + back + gy_copies + gz_copies + ga_copies:
+    for copy in sum(fwd + back, []) + early + gy_copies + gz_copies + ga_copies:
         copy.wait_send()
 
 
@@ -399,8 +503,21 @@
     slab = 2 * width // ny
     dma = pltpu.SemaphoreType.DMA
     vmem = pl.BlockSpec(memory_space=pltpu.VMEM)
-    smem = pl.BlockSpec(memory_space=pltpu.SMEM)
+    anywhere = pl.BlockSpec(memory_space=pl.ANY)
     blocks = (nb, width, blk)
+    args = (
+        local_dst,
+        local_src,
+        remote_dst.transpose(1, 0, 2),
+        remote_src.transpose(1, 0, 2),
+        features.T,
+        cotangent.T,
+        w_self,
+        w_neigh,
+        degree.reshape(1, rows),
+        local_vals[0],
+        remote_vals[0],
+    )
     out, gx, gs, gn = pl.pallas_call(
         functools.partial(kernel, nd, nf, offsets),
         out_shape=(
@@ -409,9 +526,13 @@
             jax.ShapeDtypeStruct((width, wide), F32),
             jax.ShapeDtypeStruct((width, wide), F32),
         ),
-        in_specs=[smem] * 4 + [vmem] * 7,
+        in_specs=[anywhere] * 11,
         out_specs=(vmem,) * 4,
         scratch_shapes=[
+            pltpu.SMEM(a.shape, jnp.int32) if k < 4 else pltpu.VMEM(a.shape, a.dtype)
+            for k, a in enumerate(args)
+        ]
+        + [
             pltpu.VMEM(blocks, BF16),
             pltpu.VMEM((2,) + blocks, F32),
             pltpu.VMEM(blocks, F32),
@@ -433,18 +554,17 @@
             pltpu.VMEM((Z_CHIPS, slab, wide), BF16),
             pltpu.VMEM((ny, slab, wide), BF16),
             pltpu.VMEM((width, rows), F32),
-            dma((6,)),
-            dma((6,)),
-            dma((6,)),
-            dma((6,)),
+            dma((len(args),)),
+            dma((rounds,)),
+            dma((6, CUTS)),
+            dma((6, CUTS)),
+            dma((6, CUTS)),
+            dma((6, CUTS)),
             dma((nf,)),
             dma((nf,)),
-            dma((nf,)),
-            dma((nf,)),
-            dma((9,)),
-            dma((9,)),
-            dma((9,)),
-            dma((9,)),
+        ]
+        + [dma((21,))] * 6
+        + [
             dma((ny,)),
             dma((ny,)),
             dma((Z_CHIPS,)),
@@ -453,21 +573,9 @@
             dma((ny,)),
         ],
         compiler_params=pltpu.CompilerParams(
-            collective_id=0, has_side_effects=True, vmem_limit_bytes=40 * 1024 * 1024
+            collective_id=0, has_side_effects=True, vmem_limit_bytes=60 * 1024 * 1024
         ),
-    )(
-        local_dst,
-        local_src,
-        remote_dst[0],
-        remote_src[0],
-        features.T,
-        cotangent.T,
-        w_self,
-        w_neigh,
-        degree.reshape(1, rows),
-        local_vals[0],
-        remote_vals[0],
-    )
+    )(*args)
     return out.T, gx.T, gs, gn
 
 

time: 116 us -> 103 us (0.89)
  the two profiles are of different devices: /device:TPU:66 before, /device:TPU:1 now
where the time goes in v2:
time: 103 us; the launch traced here: 102 us
  Pallas kernels  95.3 us (93%)
  local copies, waits for them, and re-layouts  6.37 us (6%)
    pallas_call x1, Pallas kernels, body(): pl.pallas_call(functools.partial(kernel, nd, nf, offsets), out_shape=(jax...  95.3 us
    unnamed x4, local copies, waits for them, and re-layouts  6.37 us

profile of v2, /device:TPU:1, one launch (start us, length us, event | category | flops | bytes accessed | tf_op | source)
XLA Modules:
  0.0 102.3 jit_solution(957750799304504129)
XLA Ops:
  0.6 95.3 %shard_map.138 = (bf16[64,1024]{1,0:T(8,128)(2,1)}, f32[64,1024]{1,0:T(8,128)}, f32[64,512]{1,0:T(8,128)}, f32[64,512]{1,0:T(8,128)}) custom-call(s32[1,16]{1,0:T(1,128)} %refs_0_.1, s32[1,16]{1,0:T(1,128)} %refs_1_.1, s32[6,1,8]{2,1,0:T(1,128)} %bitcast.16, s32[6,1,8]{2,1,0:T(1,128)} %bitcast.17, bf16[64,1024]{1,0:T(8,128)(2,1)} %bitcast.13, ...), custom_call_target="tpu_custom_call" | custom-call | tf_op jit(solution)/shard_map/pallas_call | solution.py:521
  95.9 1.6 %copy.19 = bf16[1024,64]{0,1:T(8,128)(2,1)} copy(bf16[1024,64]{0,1:T(8,128)(2,1)} %bitcast.12) | data formatting | bytes 262144
  97.5 1.7 %copy.20 = f32[1024,64]{0,1:T(8,128)} copy(f32[1024,64]{0,1:T(8,128)} %bitcast.11) | data formatting | bytes 524288
  99.2 1.6 %copy.21 = f32[64,512]{1,0:T(8,128)} copy(f32[64,512]{1,0:T(8,128)} %get-tuple-element.18) | data formatting | bytes 262144
  100.7 1.6 %copy.22 = f32[64,512]{1,0:T(8,128)} copy(f32[64,512]{1,0:T(8,128)} %get-tuple-element.19) | data formatting | bytes 262144

commit v3 on v2

--- a/solution.py
+++ b/solution.py
@@ -10,6 +10,7 @@
 Z_CHIPS = 12
 CORES = 2
 CUTS = 2
+Z_GROUP = 4
 MESH = pl.DeviceIdType.MESH
 F32 = jnp.float32
 BF16 = jnp.bfloat16
@@ -27,8 +28,7 @@
         parts,
         psend,
         precv,
-        wt,
-        wrecv,
+        wfull,
         wsn,
         xfull,
         afull,
@@ -43,6 +43,7 @@
         gsend,
         gyrecv,
         gz,
+        gg,
         gfin,
         pre,
         load_in,
@@ -63,6 +64,8 @@
         gyr,
         gzs,
         gzr,
+        ggs,
+        ggr,
         gas,
         gar,
     ) = refs
@@ -111,9 +114,13 @@
     barrier = pltpu.get_barrier_semaphore()
     near = sorted({h % nd for h in up + down} | {(nd - h) % nd for h in up + down})
     partners = [(dom_at(h), f) for h in near]
-    partners += [(me, (f + k) % nf) for k in range(1, nf)]
-    partners += [(y * nz + (z + k) % nz, f) for k in range(1, nz)]
-    partners += [(((y + k) % ny) * nz + z, f) for k in range(1, ny)]
+    partners += [(me, to) for to in ((f_sib, f_left, f_right) if nx > 1 else (f_sib,))]
+    nzg = nz // Z_GROUP
+    zg, zl = z // Z_GROUP, z % Z_GROUP
+    in_group = [y * nz + zg * Z_GROUP + (zl + k) % Z_GROUP for k in range(1, Z_GROUP)]
+    over_groups = [y * nz + ((zg + k) % nzg) * Z_GROUP + zl for k in range(1, nzg)]
+    over_y = [((y + k) % ny) * nz + z for k in range(1, ny)]
+    partners += [(to, f) for to in in_group + over_groups + over_y]
     for partner in partners:
         pl.semaphore_signal(barrier, inc=1, device_id=partner, device_id_type=MESH)
 
@@ -178,59 +185,49 @@
             for j in range(CUTS)
         ]
 
-    quarter = width // 4
-
     class Ring:
 
         def __init__(self, full, send, recv):
             self.full, self.send, self.recv = full, send, recv
-            self.copies, self.used = [], 0
-
-        def go(self, which, feat, low, parts_):
-            part = self.full.at[which, pl.ds(low * quarter, parts_ * quarter)]
-            k = self.used
-            self.used += 1
+            self.copies, self.half = [], full.shape[1] // 2
+
+        def go(self, which, feat, low, halves):
+            part = self.full.at[which, pl.ds(low * self.half, halves * self.half)]
+            k = len(self.copies)
             copy = push(part, part, self.send.at[k], self.recv.at[k], me, feat)
             self.copies.append(copy)
             return copy
 
         def start(self):
             if nx > 1:
-                self.left, self.right = {}, {}
-                for low, high in ((0, 2), (1, 3), (2, 0), (3, 1)):
+                self.left, self.right = [None] * 2, [None] * 2
+                for low in (0, 1):
                     self.left[low] = self.go(f, f_right, low, 1)
-                    self.right[high] = self.go(f, f_left, high, 1)
-            self.sib = [self.go(f, f_sib, 0, 4)]
+                    self.right[1 - low] = self.go(f, f_left, 1 - low, 1)
+            self.sib = [self.go(f, f_sib, 0, 2)]
 
         def middle(self):
             if nx == 1:
                 return
-            self.opp = []
-            for low in (0, 1):
-                self.left[low].wait_recv()
-                self.opp.append((low, self.go(f_left, f_right, low, 1)))
-                self.right[low + 2].wait_recv()
-                self.opp.append((low + 2, self.go(f_right, f_left, low + 2, 1)))
+            self.left[0].wait_recv()
+            self.opp = [self.go(f_left, f_right, 0, 1)]
+            self.right[1].wait_recv()
+            self.opp.append(self.go(f_right, f_left, 1, 1))
+            self.left[1].wait_recv()
             self.sib.append(self.go(f_left, f_sib, 0, 2))
-            self.sib.append(self.go(f_right, f_sib, 2, 2))
-            for low in (2, 3):
-                self.left[low].wait_recv()
-                self.right[low - 2].wait_recv()
-            self.sib.append(self.go(f_left, f_sib, 2, 2))
+            self.right[0].wait_recv()
             self.sib.append(self.go(f_right, f_sib, 0, 2))
 
         def last(self):
             if nx == 1:
                 return
-            for low, copy in self.opp:
-                copy.wait_recv()
+            for low in (0, 1):
+                self.opp[low].wait_recv()
                 self.sib.append(self.go(f_opp, f_sib, low, 1))
 
         def finish(self):
             for copy in self.sib:
                 copy.wait_recv()
-            for copy in self.copies:
-                copy.wait_send()
 
     ready(2, 3, 4)
     for b in range(nb):
@@ -253,14 +250,9 @@
         cols = jnp.concatenate(
             [ws[:, q * blk : (q + 1) * blk], wn[:, q * blk : (q + 1) * blk]], axis=0
         )
-        turned = cols.T
-        for h in range(blk // width):
-            wt[q * (blk // width) + h] = turned[h * width : (h + 1) * width]
-    wrecv[f] = wt[f]
-    early = []
-    for k in range(1, nf):
-        to = (f + k) % nf
-        early.append(push(wt.at[to], wrecv.at[f], wss.at[k], wsr.at[k], me, to))
+        wfull[f, q * blk : (q + 1) * blk] = cols.T
+    w_ring = Ring(wfull, wss, wsr)
+    w_ring.start()
 
     ready(("rv", 1), ("rv", 4))
     remote_forward(1, to_acc(0))
@@ -288,11 +280,13 @@
 
     add_on(2, (up[1], -down[1]))
     x_ring.middle()
+    w_ring.middle()
     ready(("rv", 0), ("rv", 5))
     remote_forward(0, to_acc(0))
     remote_forward(5, to_acc(1))
     add_on(4, (up[2], -down[2]))
     x_ring.last()
+    w_ring.last()
     ready(0, 1, 9)
 
     def to_loc(b, total):
@@ -311,14 +305,14 @@
             (((1,), (1,)), ((), ())),
             add_loc if g else to_loc,
         )
-    for copy in early:
-        copy.wait_recv()
     x_ring.finish()
+    w_ring.finish()
     pair = blk // width
-    for half, dst in ((0, 0), (1, 1)):
+    mine = [wfull[g, pl.ds(f * width, width)] for g in range(nf)]
+    for half in (0, 1):
         for q in range(nf // pair):
-            wsn[dst, :, q * blk : (q + 1) * blk] = jnp.concatenate(
-                [wrecv[q * pair + h][:, half * width : (half + 1) * width] for h in range(pair)],
+            wsn[half, :, q * blk : (q + 1) * blk] = jnp.concatenate(
+                [g[:, half * width : (half + 1) * width] for g in mine[q * pair : (q + 1) * pair]],
                 axis=1,
             )
     pre[...] = jnp.dot(
@@ -326,38 +320,44 @@
     )
     ready(8, 5)
     inverse = 1.0 / deg[...].astype(F32)
-    for j in range(CUTS):
+    a_rings = [Ring(afull.at[j], as_.at[j], ar.at[j]) for j in range(CUTS)]
+    d_rings = [Ring(dfull.at[j], ds.at[j], dr.at[j]) for j in range(CUTS)]
+    run = span * blk
+
+    def aggregate(j):
         fwd[4][j].wait_recv()
         fwd[5][j].wait_recv()
-        for b in range(j * span, (j + 1) * span):
-            sums = loc[b] + precv[4, b].astype(F32) + precv[5, b].astype(F32)
-            afull[f, :, b * blk : (b + 1) * blk] = (
-                sums * inverse[:, b * blk : (b + 1) * blk]
+        for b in range(span):
+            k = j * span + b
+            sums = loc[k] + precv[4, k].astype(F32) + precv[5, k].astype(F32)
+            afull[j, f, :, b * blk : (b + 1) * blk] = (
+                sums * inverse[:, k * blk : (k + 1) * blk]
             ).astype(BF16)
-
-    def gather(full, send, recv):
-        ring = Ring(full, send, recv)
-        ring.start()
-        ring.middle()
-        ring.last()
-        ring.finish()
-
-    gather(afull, as_, ar)
-    total = pre[...] + jnp.dot(
-        wsn[1], afull[...].reshape(nf * width, rows), preferred_element_type=F32
-    )
-    sigma = 1.0 / (1.0 + jnp.exp(-total))
-    out[...] = (total * sigma).astype(BF16)
-    dfull[f] = (ct[...].astype(F32) * sigma * (1.0 + total * (1.0 - sigma))).astype(BF16)
-
-    gather(dfull, ds, dr)
-    dall = dfull[...].reshape(nf * width, rows)
+        a_rings[j].start()
+
+    def activate(j):
+        a_rings[j].finish()
+        low, high = j * run, (j + 1) * run
+        total = pre[:, low:high] + jnp.dot(
+            wsn[1], afull[j].reshape(nf * width, run), preferred_element_type=F32
+        )
+        sigma = 1.0 / (1.0 + jnp.exp(-total))
+        dfull[j, f] = (
+            ct[:, low:high].astype(F32) * sigma * (1.0 + total * (1.0 - sigma))
+        ).astype(BF16)
+        d_rings[j].start()
+        out[:, low:high] = (total * sigma).astype(BF16)
+
     back = [[], []] + [None] * 4
     back_down = [o[0], o[1] - o[0], o[2] - o[1]]
     back_up = [nd - o[5], o[5] - o[4], o[4] - o[3]]
-    for j in range(CUTS):
-        low, high = j * span * blk, (j + 1) * span * blk
-        dagg = jnp.dot(wn[...], dall[:, low:high], preferred_element_type=F32)
+
+    def turn(j):
+        d_rings[j].finish()
+        low, high = j * run, (j + 1) * run
+        dagg = jnp.dot(
+            wn[...], dfull[j].reshape(nf * width, run), preferred_element_type=F32
+        )
         dagg = dagg * inverse[:, low:high]
         for b in range(span):
             dsb[j * span + b] = dagg[:, b * blk : (b + 1) * blk].astype(BF16)
@@ -374,12 +374,29 @@
                 )
             )
 
-    grad = lax.dot_general(
-        jnp.concatenate([xt[...], afull[f]], axis=0),
-        dall,
-        (((1,), (1,)), ((), ())),
-        preferred_element_type=F32,
-    )
+    aggregate(0)
+    aggregate(1)
+    a_rings[0].middle()
+    a_rings[0].last()
+    a_rings[1].middle()
+    activate(0)
+    a_rings[1].last()
+    activate(1)
+    d_rings[0].middle()
+    d_rings[0].last()
+    d_rings[1].middle()
+    turn(0)
+    d_rings[1].last()
+    turn(1)
+
+    grad = jnp.zeros((2 * width, nf * width), F32)
+    for j in range(CUTS):
+        grad = grad + lax.dot_general(
+            jnp.concatenate([xt[:, j * run : (j + 1) * run], afull[j, f]], axis=0),
+            dfull[j].reshape(nf * width, run),
+            (((1,), (1,)), ((), ())),
+            preferred_element_type=F32,
+        )
     slab = gsend.shape[1]
     for k in range(ny):
         gsend[k] = grad[k * slab : (k + 1) * slab].astype(BF16)
@@ -391,7 +408,10 @@
             push(gsend.at[to], gyrecv.at[y], gys.at[k], gyr.at[k], to * nz + z, f)
         )
 
-    gx[...] = jnp.dot(ws[...], dall, preferred_element_type=F32)
+    for j in range(CUTS):
+        gx[:, j * run : (j + 1) * run] = jnp.dot(
+            ws[...], dfull[j].reshape(nf * width, run), preferred_element_type=F32
+        )
 
     def add_gx(b, total):
         gx[:, b * blk : (b + 1) * blk] = gx[:, b * blk : (b + 1) * blk] + total
@@ -419,54 +439,60 @@
             add_gx,
         )
 
-    def relay(k, by):
-        for j in range(CUTS):
-            part = pl.ds(j * span, span)
-            for side in (0, 1):
-                n = k + 2 + side
-                back[k + side][j].wait_recv()
-                if by is None:
-                    continue
-                if j == 0:
-                    back[n] = []
-                back[n].append(
-                    push(
-                        drecv[k + side].at[part],
-                        drecv[n].at[part],
-                        bs.at[n, j],
-                        br.at[n, j],
-                        dom_at(by[side]),
-                        f,
-                    )
+    def relay(k, j, by):
+        part = pl.ds(j * span, span)
+        for side in (0, 1):
+            n = k + 2 + side
+            back[k + side][j].wait_recv()
+            if by is None:
+                continue
+            if j == 0:
+                back[n] = []
+            back[n].append(
+                push(
+                    drecv[k + side].at[part],
+                    drecv[n].at[part],
+                    bs.at[n, j],
+                    br.at[n, j],
+                    dom_at(by[side]),
+                    f,
                 )
-
-    relay(0, (-back_down[1], back_up[1]))
+            )
+
+    def summed(ref):
+        total = ref[0].astype(F32)
+        for k in range(1, ref.shape[0]):
+            total = total + ref[k].astype(F32)
+        return total.astype(BF16)
+
+    def share(ref, slot, devices, send, recv):
+        return [
+            push(ref.at[slot], ref.at[slot], send.at[k], recv.at[k], to, f)
+            for k, to in enumerate(devices)
+        ]
+
+    relay(0, 0, (-back_down[1], back_up[1]))
     for copy in gy_copies:
         copy.wait_recv()
-    mine = gyrecv[0].astype(F32)
-    for k in range(1, ny):
-        mine = mine + gyrecv[k].astype(F32)
-    gz[z] = mine.astype(BF16)
-    gz_copies = []
-    for k in range(1, nz):
-        to = (z + k) % nz
-        gz_copies.append(push(gz.at[z], gz.at[z], gzs.at[k], gzr.at[k], y * nz + to, f))
+    gz[zl] = summed(gyrecv)
+    gz_copies = share(gz, zl, in_group, gzs, gzr)
+    relay(0, 1, (-back_down[1], back_up[1]))
     remote_back(0, 0)
     remote_back(5, 1)
-    relay(2, (-back_down[2], back_up[2]))
+    for copy in gz_copies:
+        copy.wait_recv()
+    gg[zg] = summed(gz)
+    gg_copies = share(gg, zg, over_groups, ggs, ggr)
+    relay(2, 0, (-back_down[2], back_up[2]))
+    relay(2, 1, (-back_down[2], back_up[2]))
     remote_back(1, 2)
     remote_back(4, 3)
-    for copy in gz_copies:
+    for copy in gg_copies:
         copy.wait_recv()
-    mine = gz[0].astype(F32)
-    for k in range(1, nz):
-        mine = mine + gz[k].astype(F32)
-    gfin[y] = mine.astype(BF16)
-    ga_copies = []
-    for k in range(1, ny):
-        to = (y + k) % ny
-        ga_copies.append(push(gfin.at[y], gfin.at[y], gas.at[k], gar.at[k], to * nz + z, f))
-    relay(4, None)
+    gfin[y] = summed(gg)
+    ga_copies = share(gfin, y, over_y, gas, gar)
+    relay(4, 0, None)
+    relay(4, 1, None)
     remote_back(2, 4)
     remote_back(3, 5)
     for copy in ga_copies:
@@ -474,8 +500,20 @@
     result = gfin[...].reshape(2 * width, gfin.shape[2]).astype(F32)
     gs[...] = result[:width]
     gn[...] = result[width:]
-    for copy in sum(fwd + back, []) + early + gy_copies + gz_copies + ga_copies:
+    rings = [x_ring, w_ring] + a_rings + d_rings
+    for copy in sum(fwd + back + [ring.copies for ring in rings], []):
         copy.wait_send()
+    for copy in gy_copies + gz_copies + gg_copies + ga_copies:
+        copy.wait_send()
+
+
+def write_out(*refs):
+    n = len(refs) // 2
+    copies = [pltpu.make_async_copy(refs[k], refs[n + k], refs[2 * n].at[k]) for k in range(n)]
+    for copy in copies:
+        copy.start()
+    for copy in copies:
+        copy.wait()
 
 
 def body(
@@ -503,7 +541,7 @@
     slab = 2 * width // ny
     dma = pltpu.SemaphoreType.DMA
     vmem = pl.BlockSpec(memory_space=pltpu.VMEM)
-    anywhere = pl.BlockSpec(memory_space=pl.ANY)
+    hbm = pl.BlockSpec(memory_space=pltpu.HBM)
     blocks = (nb, width, blk)
     args = (
         local_dst,
@@ -518,7 +556,7 @@
         local_vals[0],
         remote_vals[0],
     )
-    out, gx, gs, gn = pl.pallas_call(
+    results = pl.pallas_call(
         functools.partial(kernel, nd, nf, offsets),
         out_shape=(
             jax.ShapeDtypeStruct((width, rows), BF16),
@@ -526,7 +564,7 @@
             jax.ShapeDtypeStruct((width, wide), F32),
             jax.ShapeDtypeStruct((width, wide), F32),
         ),
-        in_specs=[anywhere] * 11,
+        in_specs=[hbm] * 11,
         out_specs=(vmem,) * 4,
         scratch_shapes=[
             pltpu.SMEM(a.shape, jnp.int32) if k < 4 else pltpu.VMEM(a.shape, a.dtype)
@@ -539,19 +577,19 @@
             pltpu.VMEM((per, width, blk), F32),
             pltpu.VMEM((6,) + blocks, BF16),
             pltpu.VMEM((6,) + blocks, BF16),
-            pltpu.VMEM((nf, width, 2 * width), BF16),
-            pltpu.VMEM((nf, width, 2 * width), BF16),
+            pltpu.VMEM((nf, wide, 2 * width), BF16),
             pltpu.VMEM((2, width, nf * width), BF16),
             pltpu.VMEM((nf, width, rows), BF16),
-            pltpu.VMEM((nf, width, rows), BF16),
-            pltpu.VMEM((nf, width, rows), BF16),
+            pltpu.VMEM((CUTS, nf, width, rows // CUTS), BF16),
+            pltpu.VMEM((CUTS, nf, width, rows // CUTS), BF16),
             pltpu.VMEM(blocks, BF16),
         ]
         + [pltpu.VMEM(blocks, BF16)] * 6
         + [
             pltpu.VMEM((ny, slab, wide), BF16),
             pltpu.VMEM((ny, slab, wide), BF16),
-            pltpu.VMEM((Z_CHIPS, slab, wide), BF16),
+            pltpu.VMEM((Z_GROUP, slab, wide), BF16),
+            pltpu.VMEM((Z_CHIPS // Z_GROUP, slab, wide), BF16),
             pltpu.VMEM((ny, slab, wide), BF16),
             pltpu.VMEM((width, rows), F32),
             dma((len(args),)),
@@ -560,15 +598,16 @@
             dma((6, CUTS)),
             dma((6, CUTS)),
             dma((6, CUTS)),
-            dma((nf,)),
-            dma((nf,)),
         ]
-        + [dma((21,))] * 6
+        + [dma((11,))] * 4
+        + [dma((CUTS, 11))] * 4
         + [
             dma((ny,)),
             dma((ny,)),
-            dma((Z_CHIPS,)),
-            dma((Z_CHIPS,)),
+            dma((Z_GROUP,)),
+            dma((Z_GROUP,)),
+            dma((Z_CHIPS // Z_GROUP,)),
+            dma((Z_CHIPS // Z_GROUP,)),
             dma((ny,)),
             dma((ny,)),
         ],
@@ -576,6 +615,14 @@
             collective_id=0, has_side_effects=True, vmem_limit_bytes=60 * 1024 * 1024
         ),
     )(*args)
+    out, gx, gs, gn = pl.pallas_call(
+        write_out,
+        out_shape=tuple(jax.ShapeDtypeStruct(r.shape, r.dtype) for r in results),
+        in_specs=[hbm] * 4,
+        out_specs=(hbm,) * 4,
+        scratch_shapes=[dma((4,))],
+        compiler_params=pltpu.CompilerParams(vmem_limit_bytes=60 * 1024 * 1024),
+    )(*results)
     return out.T, gx.T, gs, gn
 
 

time: 103 us -> 118 us (1.15)
  Pallas kernels: 95.3 us -> 117 us
  local copies, waits for them, and re-layouts: 6.37 us -> 0 us
    pallas_call x0 -> x1, Pallas kernels: none -> 21 us  [body(): pl.pallas_call(write_out, out_shape=tuple((jax.ShapeDtypeStruct(r.shape,...]
    unnamed x4 -> x0, local copies, waits for them, and re-layouts: 6.37 us -> none
where the time goes in v3:
time: 118 us
  Pallas kernels  117 us (99%)
    pallas_call x1, Pallas kernels, body(): pl.pallas_call(functools.partial(kernel, nd, nf, offsets), out_shape=(jax...  96 us
    pallas_call x1, Pallas kernels, body(): pl.pallas_call(write_out, out_shape=tuple((jax.ShapeDtypeStruct(r.shape,...  21 us

profile of v3, /device:TPU:1, one launch (start us, length us, event | category | flops | bytes accessed | tf_op | source)
XLA Modules:
  0.0 117.6 jit_solution(1457487803117971759)
XLA Ops:
  0.6 96.0 %shard_map.138 = (bf16[64,1024]{1,0:T(8,128)(2,1)}, f32[64,1024]{1,0:T(8,128)}, f32[64,512]{1,0:T(8,128)}, f32[64,512]{1,0:T(8,128)}) custom-call(s32[1,16]{1,0:T(1,128)} %refs_0_.1, s32[1,16]{1,0:T(1,128)} %refs_1_.1, s32[6,1,8]{2,1,0:T(1,128)} %bitcast.14, s32[6,1,8]{2,1,0:T(1,128)} %bitcast.15, bf16[64,1024]{1,0:T(8,128)(2,1)} %bitcast.11, ...), custom_call_target="tpu_custom_call" | custom-call | tf_op jit(solution)/shard_map/pallas_call | solution.py:559
  96.7 21.0 %shard_map.139 = (bf16[64,1024]{1,0:T(8,128)(2,1)}, f32[64,1024]{1,0:T(8,128)}, f32[64,512]{1,0:T(8,128)}, f32[64,512]{1,0:T(8,128)}) custom-call(bf16[64,1024]{1,0:T(8,128)(2,1)} %get-tuple-element.12.refs_0_, f32[64,1024]{1,0:T(8,128)} %get-tuple-element.13.refs_1_, f32[64,512]{1,0:T(8,128)} %get-tuple-element.14.refs_2_, f32[64,512]{1,0:T(8,128)} %get-tuple-element.15.refs_3_), custom_call_target="tpu_custom_call" | custom-call | tf_op jit(solution)/shard_map/pallas_call | solution.py:618

commit v4 on v3

--- a/solution.py
+++ b/solution.py
@@ -28,11 +28,21 @@
         parts,
         psend,
         precv,
-        wfull,
-        wsn,
-        xfull,
-        afull,
+        xw,
+        xz,
+        cw,
+        cz,
+        wall,
+        wt,
+        asend,
+        az,
+        aggt,
+        osend,
+        ow,
+        dsend,
+        dw,
         dfull,
+        dall,
         dsb,
         dr0,
         dr1,
@@ -54,12 +64,18 @@
         br,
         wss,
         wsr,
+        ds,
+        dr,
         xs,
         xr,
+        cs,
+        cr,
         as_,
         ar,
-        ds,
-        dr,
+        os_,
+        or_,
+        es,
+        er,
         gys,
         gyr,
         gzs,
@@ -114,7 +130,7 @@
     barrier = pltpu.get_barrier_semaphore()
     near = sorted({h % nd for h in up + down} | {(nd - h) % nd for h in up + down})
     partners = [(dom_at(h), f) for h in near]
-    partners += [(me, to) for to in ((f_sib, f_left, f_right) if nx > 1 else (f_sib,))]
+    partners += [(me, (f + k) % nf) for k in range(1, nf)]
     nzg = nz // Z_GROUP
     zg, zl = z // Z_GROUP, z % Z_GROUP
     in_group = [y * nz + zg * Z_GROUP + (zl + k) % Z_GROUP for k in range(1, Z_GROUP)]
@@ -229,30 +245,42 @@
             for copy in self.sib:
                 copy.wait_recv()
 
+    wide = rows // nf
+    per_dev = wide // blk
+
+    def exchange(src, dst, send, recv):
+        dst[f] = src[f]
+        return [
+            push(src.at[(f + k) % nf], dst.at[f], send.at[k], recv.at[k], me, (f + k) % nf)
+            for k in range(1, nf)
+        ]
+
+    def arrive(copies):
+        for copy in copies:
+            copy.wait_recv()
+
     ready(2, 3, 4)
     for b in range(nb):
         xb[b] = xt[:, b * blk : (b + 1) * blk]
-    xfull[f] = xt[...]
     ready(("rv", 2))
     remote_forward(2, to_send(0))
+    pl.semaphore_wait(barrier, len(partners))
+    fwd = [None] * 6
+    fwd[0] = hop(psend.at[0], precv.at[0], fs, fr, 0, up[0])
     ready(("rv", 3))
     remote_forward(3, to_send(1))
-    pl.semaphore_wait(barrier, len(partners))
-
-    fwd = [None] * 6
-    fwd[0] = hop(psend.at[0], precv.at[0], fs, fr, 0, up[0])
     fwd[1] = hop(psend.at[1], precv.at[1], fs, fr, 1, -down[0])
 
-    x_ring = Ring(xfull, xs, xr)
-    x_ring.start()
-    ready(6, 7)
-    for q in range(ws.shape[1] // blk):
-        cols = jnp.concatenate(
-            [ws[:, q * blk : (q + 1) * blk], wn[:, q * blk : (q + 1) * blk]], axis=0
-        )
-        wfull[f, q * blk : (q + 1) * blk] = cols.T
-    w_ring = Ring(wfull, wss, wsr)
+    ready(6, 7, 5)
+    wall[f, :width] = ws[...]
+    wall[f, width:] = wn[...]
+    w_ring = Ring(wall, wss, wsr)
     w_ring.start()
+    for g in range(nf):
+        xw[g] = xt[:, g * wide : (g + 1) * wide]
+        cw[g] = ct[:, g * wide : (g + 1) * wide]
+    x_copies = exchange(xw, xz, xs, xr)
+    c_copies = exchange(cw, cz, cs, cr)
 
     ready(("rv", 1), ("rv", 4))
     remote_forward(1, to_acc(0))
@@ -279,13 +307,11 @@
                 )
 
     add_on(2, (up[1], -down[1]))
-    x_ring.middle()
     w_ring.middle()
     ready(("rv", 0), ("rv", 5))
     remote_forward(0, to_acc(0))
     remote_forward(5, to_acc(1))
     add_on(4, (up[2], -down[2]))
-    x_ring.last()
     w_ring.last()
     ready(0, 1, 9)
 
@@ -305,98 +331,68 @@
             (((1,), (1,)), ((), ())),
             add_loc if g else to_loc,
         )
-    x_ring.finish()
     w_ring.finish()
     pair = blk // width
-    mine = [wfull[g, pl.ds(f * width, width)] for g in range(nf)]
     for half in (0, 1):
         for q in range(nf // pair):
-            wsn[half, :, q * blk : (q + 1) * blk] = jnp.concatenate(
-                [g[:, half * width : (half + 1) * width] for g in mine[q * pair : (q + 1) * pair]],
-                axis=1,
+            rows_in = jnp.concatenate(
+                [wall[q * pair + h, half * width : (half + 1) * width] for h in range(pair)], axis=0
             )
-    pre[...] = jnp.dot(
-        wsn[0], xfull[...].reshape(nf * width, rows), preferred_element_type=F32
+            wt[half, :, q * blk : (q + 1) * blk] = rows_in.T
+    arrive(x_copies)
+    pre[...] = jnp.dot(wt[0], xz[...].reshape(nf * width, wide), preferred_element_type=F32)
+    arrive(c_copies)
+    ready(8)
+    inverse = 1.0 / deg[...].astype(F32)
+    for j in range(CUTS):
+        arrive([fwd[4][j], fwd[5][j]])
+        for b in range(j * span, (j + 1) * span):
+            sums = loc[b] + precv[4, b].astype(F32) + precv[5, b].astype(F32)
+            piece = (sums * inverse[:, b * blk : (b + 1) * blk]).astype(BF16)
+            aggt[:, b * blk : (b + 1) * blk] = piece
+            at = (b % per_dev) * blk
+            asend[b // per_dev, :, at : at + blk] = piece
+    a_copies = exchange(asend, az, as_, ar)
+    arrive(a_copies)
+    total = pre[...] + jnp.dot(
+        wt[1], az[...].reshape(nf * width, wide), preferred_element_type=F32
     )
-    ready(8, 5)
-    inverse = 1.0 / deg[...].astype(F32)
-    a_rings = [Ring(afull.at[j], as_.at[j], ar.at[j]) for j in range(CUTS)]
-    d_rings = [Ring(dfull.at[j], ds.at[j], dr.at[j]) for j in range(CUTS)]
-    run = span * blk
-
-    def aggregate(j):
-        fwd[4][j].wait_recv()
-        fwd[5][j].wait_recv()
-        for b in range(span):
-            k = j * span + b
-            sums = loc[k] + precv[4, k].astype(F32) + precv[5, k].astype(F32)
-            afull[j, f, :, b * blk : (b + 1) * blk] = (
-                sums * inverse[:, k * blk : (k + 1) * blk]
-            ).astype(BF16)
-        a_rings[j].start()
-
-    def activate(j):
-        a_rings[j].finish()
-        low, high = j * run, (j + 1) * run
-        total = pre[:, low:high] + jnp.dot(
-            wsn[1], afull[j].reshape(nf * width, run), preferred_element_type=F32
-        )
-        sigma = 1.0 / (1.0 + jnp.exp(-total))
-        dfull[j, f] = (
-            ct[:, low:high].astype(F32) * sigma * (1.0 + total * (1.0 - sigma))
-        ).astype(BF16)
-        d_rings[j].start()
-        out[:, low:high] = (total * sigma).astype(BF16)
+    sigma = 1.0 / (1.0 + jnp.exp(-total))
+    dpre = (
+        cz[...].reshape(nf * width, wide).astype(F32) * sigma * (1.0 + total * (1.0 - sigma))
+    ).astype(BF16)
+    own = 1.0 / deg[:, pl.ds(pl.multiple_of(f * wide, blk), wide)].astype(F32)
+    dagg = jnp.dot(
+        wall[:, width:, :].reshape(nf * width, nf * width), dpre, preferred_element_type=F32
+    )
+    dsend[...] = (dagg * own).astype(BF16).reshape(nf, width, wide)
+    e_copies = exchange(dsend, dw, es, er)
+    dfull[f] = dpre
+    d_ring = Ring(dfull, ds, dr)
+    d_ring.start()
+    osend[...] = (total * sigma).astype(BF16).reshape(nf, width, wide)
+    o_copies = exchange(osend, ow, os_, or_)
 
     back = [[], []] + [None] * 4
     back_down = [o[0], o[1] - o[0], o[2] - o[1]]
     back_up = [nd - o[5], o[5] - o[4], o[4] - o[3]]
-
-    def turn(j):
-        d_rings[j].finish()
-        low, high = j * run, (j + 1) * run
-        dagg = jnp.dot(
-            wn[...], dfull[j].reshape(nf * width, run), preferred_element_type=F32
-        )
-        dagg = dagg * inverse[:, low:high]
-        for b in range(span):
-            dsb[j * span + b] = dagg[:, b * blk : (b + 1) * blk].astype(BF16)
-        part = pl.ds(j * span, span)
-        for side, by in ((0, -back_down[0]), (1, back_up[0])):
-            back[side].append(
-                push(
-                    dsb.at[part],
-                    drecv[side].at[part],
-                    bs.at[side, j],
-                    br.at[side, j],
-                    dom_at(by),
-                    f,
-                )
-            )
-
-    aggregate(0)
-    aggregate(1)
-    a_rings[0].middle()
-    a_rings[0].last()
-    a_rings[1].middle()
-    activate(0)
-    a_rings[1].last()
-    activate(1)
-    d_rings[0].middle()
-    d_rings[0].last()
-    d_rings[1].middle()
-    turn(0)
-    d_rings[1].last()
-    turn(1)
-
-    grad = jnp.zeros((2 * width, nf * width), F32)
-    for j in range(CUTS):
-        grad = grad + lax.dot_general(
-            jnp.concatenate([xt[:, j * run : (j + 1) * run], afull[j, f]], axis=0),
-            dfull[j].reshape(nf * width, run),
-            (((1,), (1,)), ((), ())),
-            preferred_element_type=F32,
-        )
+    arrive(e_copies)
+    for b in range(nb):
+        at = (b % per_dev) * blk
+        dsb[b] = dw[b // per_dev, :, at : at + blk]
+    back[0] = hop(dsb, drecv[0], bs, br, 0, -back_down[0])
+    back[1] = hop(dsb, drecv[1], bs, br, 1, back_up[0])
+    d_ring.middle()
+    d_ring.last()
+    d_ring.finish()
+    for g in range(nf):
+        dall[:, g * wide : (g + 1) * wide] = dfull[g]
+    grad = lax.dot_general(
+        jnp.concatenate([xt[...], aggt[...]], axis=0),
+        dall[...],
+        (((1,), (1,)), ((), ())),
+        preferred_element_type=F32,
+    )
     slab = gsend.shape[1]
     for k in range(ny):
         gsend[k] = grad[k * slab : (k + 1) * slab].astype(BF16)
@@ -408,10 +404,10 @@
             push(gsend.at[to], gyrecv.at[y], gys.at[k], gyr.at[k], to * nz + z, f)
         )
 
-    for j in range(CUTS):
-        gx[:, j * run : (j + 1) * run] = jnp.dot(
-            ws[...], dfull[j].reshape(nf * width, run), preferred_element_type=F32
-        )
+    gx[...] = jnp.dot(ws[...], dall[...], preferred_element_type=F32)
+    arrive(o_copies)
+    for g in range(nf):
+        out[:, g * wide : (g + 1) * wide] = ow[g]
 
     def add_gx(b, total):
         gx[:, b * blk : (b + 1) * blk] = gx[:, b * blk : (b + 1) * blk] + total
@@ -500,20 +496,25 @@
     result = gfin[...].reshape(2 * width, gfin.shape[2]).astype(F32)
     gs[...] = result[:width]
     gn[...] = result[width:]
-    rings = [x_ring, w_ring] + a_rings + d_rings
-    for copy in sum(fwd + back + [ring.copies for ring in rings], []):
+    for copy in sum(fwd + back + [w_ring.copies, d_ring.copies], []):
+        copy.wait_send()
+    for copy in x_copies + c_copies + a_copies + e_copies + o_copies:
         copy.wait_send()
     for copy in gy_copies + gz_copies + gg_copies + ga_copies:
         copy.wait_send()
 
 
 def write_out(*refs):
-    n = len(refs) // 2
-    copies = [pltpu.make_async_copy(refs[k], refs[n + k], refs[2 * n].at[k]) for k in range(n)]
-    for copy in copies:
-        copy.start()
-    for copy in copies:
-        copy.wait()
+    ins, outs, held, sems = refs[:4], refs[4:8], refs[8:12], refs[12]
+    fetch = [pltpu.make_async_copy(ins[k], held[k], sems.at[0, k]) for k in range(4)]
+    store = [pltpu.make_async_copy(held[k], outs[k], sems.at[1, k]) for k in range(4)]
+    for k in range(4):
+        fetch[k].start()
+    for k in range(4):
+        fetch[k].wait()
+        store[k].start()
+    for k in range(4):
+        store[k].wait()
 
 
 def body(
@@ -577,11 +578,19 @@
             pltpu.VMEM((per, width, blk), F32),
             pltpu.VMEM((6,) + blocks, BF16),
             pltpu.VMEM((6,) + blocks, BF16),
-            pltpu.VMEM((nf, wide, 2 * width), BF16),
-            pltpu.VMEM((2, width, nf * width), BF16),
-            pltpu.VMEM((nf, width, rows), BF16),
-            pltpu.VMEM((CUTS, nf, width, rows // CUTS), BF16),
-            pltpu.VMEM((CUTS, nf, width, rows // CUTS), BF16),
+        ]
+        + [pltpu.VMEM((nf, width, rows // nf), BF16)] * 4
+        + [
+            pltpu.VMEM((nf, 2 * width, wide), BF16),
+            pltpu.VMEM((2, wide, nf * width), BF16),
+            pltpu.VMEM((nf, width, rows // nf), BF16),
+            pltpu.VMEM((nf, width, rows // nf), BF16),
+            pltpu.VMEM((width, rows), BF16),
+        ]
+        + [pltpu.VMEM((nf, width, rows // nf), BF16)] * 4
+        + [
+            pltpu.VMEM((nf, wide, rows // nf), BF16),
+            pltpu.VMEM((wide, rows), BF16),
             pltpu.VMEM(blocks, BF16),
         ]
         + [pltpu.VMEM(blocks, BF16)] * 6
@@ -591,7 +600,7 @@
             pltpu.VMEM((Z_GROUP, slab, wide), BF16),
             pltpu.VMEM((Z_CHIPS // Z_GROUP, slab, wide), BF16),
             pltpu.VMEM((ny, slab, wide), BF16),
-            pltpu.VMEM((width, rows), F32),
+            pltpu.VMEM((wide, rows // nf), F32),
             dma((len(args),)),
             dma((rounds,)),
             dma((6, CUTS)),
@@ -600,7 +609,7 @@
             dma((6, CUTS)),
         ]
         + [dma((11,))] * 4
-        + [dma((CUTS, 11))] * 4
+        + [dma((nf,))] * 10
         + [
             dma((ny,)),
             dma((ny,)),
@@ -620,7 +629,7 @@
         out_shape=tuple(jax.ShapeDtypeStruct(r.shape, r.dtype) for r in results),
         in_specs=[hbm] * 4,
         out_specs=(hbm,) * 4,
-        scratch_shapes=[dma((4,))],
+        scratch_shapes=[pltpu.VMEM(r.shape, r.dtype) for r in results] + [dma((2, 4))],
         compiler_params=pltpu.CompilerParams(vmem_limit_bytes=60 * 1024 * 1024),
     )(*results)
     return out.T, gx.T, gs, gn

time: 118 us -> 89.8 us (0.76)
  Pallas kernels: 117 us -> 89 us
    pallas_call x1, Pallas kernels: 21 us -> 1.88 us  [body(): pl.pallas_call(write_out, out_shape=tuple((jax.ShapeDtypeStruct(r.shape,...]
    pallas_call x1, Pallas kernels: 96 us -> 87.1 us  [body(): pl.pallas_call(functools.partial(kernel, nd, nf, offsets), out_shape=(jax...]
where the time goes in v4:
time: 89.8 us; the launch traced here: 89.6 us
  Pallas kernels  89 us (99%)
    pallas_call x1, Pallas kernels, body(): pl.pallas_call(functools.partial(kernel, nd, nf, offsets), out_shape=(jax...  87.1 us
    pallas_call x1, Pallas kernels, body(): pl.pallas_call(write_out, out_shape=tuple((jax.ShapeDtypeStruct(r.shape,...  1.88 us

profile of v4, /device:TPU:1, one launch (start us, length us, event | category | flops | bytes accessed | tf_op | source)
XLA Modules:
  0.0 89.6 jit_solution(12616108598157207734)
XLA Ops:
  0.6 87.1 %shard_map.138 = (bf16[64,1024]{1,0:T(8,128)(2,1)}, f32[64,1024]{1,0:T(8,128)}, f32[64,512]{1,0:T(8,128)}, f32[64,512]{1,0:T(8,128)}) custom-call(s32[1,16]{1,0:T(1,128)} %refs_0_.1, s32[1,16]{1,0:T(1,128)} %refs_1_.1, s32[6,1,8]{2,1,0:T(1,128)} %bitcast.14, s32[6,1,8]{2,1,0:T(1,128)} %bitcast.15, bf16[64,1024]{1,0:T(8,128)(2,1)} %bitcast.11, ...), custom_call_target="tpu_custom_call" | custom-call | tf_op jit(solution)/shard_map/pallas_call | solution.py:560
  87.7 1.9 %shard_map.139 = (bf16[64,1024]{1,0:T(8,128)(2,1)}, f32[64,1024]{1,0:T(8,128)}, f32[64,512]{1,0:T(8,128)}, f32[64,512]{1,0:T(8,128)}) custom-call(bf16[64,1024]{1,0:T(8,128)(2,1)} %get-tuple-element.12.refs_0_, f32[64,1024]{1,0:T(8,128)} %get-tuple-element.13.refs_1_, f32[64,512]{1,0:T(8,128)} %get-tuple-element.14.refs_2_, f32[64,512]{1,0:T(8,128)} %get-tuple-element.15.refs_3_), custom_call_target="tpu_custom_call" | custom-call | tf_op jit(solution)/shard_map/pallas_call | solution.py:627

commit v5 on v4

--- a/solution.py
+++ b/solution.py
@@ -92,13 +92,6 @@
         loads[i] = pltpu.make_async_copy(ins[i], held[i], load_in.at[i])
     for key in (2, 3, 4, ("rv", 2), ("rv", 3)):
         loads[key].start()
-    for i in (0, 1, 6, 7, 9, 8, 5):
-        loads[i] = pltpu.make_async_copy(ins[i], held[i], load_in.at[i])
-    for r in (1, 4, 0, 5):
-        loads["rv", r] = pltpu.make_async_copy(ins[10].at[r], rv.at[r], load_rv.at[r])
-    for key in (6, 7, ("rv", 1), ("rv", 4), ("rv", 0), ("rv", 5), 0, 1, 9, 8, 5):
-        loads[key].start()
-
     def ready(*keys):
         for key in keys:
             loads[key].wait()
@@ -139,6 +132,13 @@
     partners += [(to, f) for to in in_group + over_groups + over_y]
     for partner in partners:
         pl.semaphore_signal(barrier, inc=1, device_id=partner, device_id_type=MESH)
+
+    for i in (0, 1, 6, 7, 9, 8, 5):
+        loads[i] = pltpu.make_async_copy(ins[i], held[i], load_in.at[i])
+    for r in (1, 4, 0, 5):
+        loads["rv", r] = pltpu.make_async_copy(ins[10].at[r], rv.at[r], load_rv.at[r])
+    for key in (6, 7, ("rv", 1), ("rv", 4), ("rv", 0), ("rv", 5), 0, 1, 9, 8, 5):
+        loads[key].start()
 
     def push(src, dst, send, recv, dom, feat):
         copy = pltpu.make_async_remote_copy(
@@ -371,7 +371,6 @@
     d_ring = Ring(dfull, ds, dr)
     d_ring.start()
     osend[...] = (total * sigma).astype(BF16).reshape(nf, width, wide)
-    o_copies = exchange(osend, ow, os_, or_)
 
     back = [[], []] + [None] * 4
     back_down = [o[0], o[1] - o[0], o[2] - o[1]]
@@ -382,8 +381,30 @@
         dsb[b] = dw[b // per_dev, :, at : at + blk]
     back[0] = hop(dsb, drecv[0], bs, br, 0, -back_down[0])
     back[1] = hop(dsb, drecv[1], bs, br, 1, back_up[0])
+    def relay(k, j, by):
+        part = pl.ds(j * span, span)
+        for side in (0, 1):
+            n = k + 2 + side
+            back[k + side][j].wait_recv()
+            if by is None:
+                continue
+            if j == 0:
+                back[n] = []
+            back[n].append(
+                push(
+                    drecv[k + side].at[part],
+                    drecv[n].at[part],
+                    bs.at[n, j],
+                    br.at[n, j],
+                    dom_at(by[side]),
+                    f,
+                )
+            )
+
+    first, second = (-back_down[1], back_up[1]), (-back_down[2], back_up[2])
     d_ring.middle()
     d_ring.last()
+    relay(0, 0, first)
     d_ring.finish()
     for g in range(nf):
         dall[:, g * wide : (g + 1) * wide] = dfull[g]
@@ -404,10 +425,10 @@
             push(gsend.at[to], gyrecv.at[y], gys.at[k], gyr.at[k], to * nz + z, f)
         )
 
+    for j in range(1, CUTS):
+        relay(0, j, first)
+    o_copies = exchange(osend, ow, os_, or_)
     gx[...] = jnp.dot(ws[...], dall[...], preferred_element_type=F32)
-    arrive(o_copies)
-    for g in range(nf):
-        out[:, g * wide : (g + 1) * wide] = ow[g]
 
     def add_gx(b, total):
         gx[:, b * blk : (b + 1) * blk] = gx[:, b * blk : (b + 1) * blk] + total
@@ -435,26 +456,6 @@
             add_gx,
         )
 
-    def relay(k, j, by):
-        part = pl.ds(j * span, span)
-        for side in (0, 1):
-            n = k + 2 + side
-            back[k + side][j].wait_recv()
-            if by is None:
-                continue
-            if j == 0:
-                back[n] = []
-            back[n].append(
-                push(
-                    drecv[k + side].at[part],
-                    drecv[n].at[part],
-                    bs.at[n, j],
-                    br.at[n, j],
-                    dom_at(by[side]),
-                    f,
-                )
-            )
-
     def summed(ref):
         total = ref[0].astype(F32)
         for k in range(1, ref.shape[0]):
@@ -467,32 +468,29 @@
             for k, to in enumerate(devices)
         ]
 
-    relay(0, 0, (-back_down[1], back_up[1]))
-    for copy in gy_copies:
-        copy.wait_recv()
+    arrive(gy_copies)
     gz[zl] = summed(gyrecv)
     gz_copies = share(gz, zl, in_group, gzs, gzr)
-    relay(0, 1, (-back_down[1], back_up[1]))
     remote_back(0, 0)
     remote_back(5, 1)
-    for copy in gz_copies:
-        copy.wait_recv()
+    for j in range(CUTS):
+        relay(2, j, second)
+    arrive(gz_copies)
     gg[zg] = summed(gz)
     gg_copies = share(gg, zg, over_groups, ggs, ggr)
-    relay(2, 0, (-back_down[2], back_up[2]))
-    relay(2, 1, (-back_down[2], back_up[2]))
     remote_back(1, 2)
     remote_back(4, 3)
-    for copy in gg_copies:
-        copy.wait_recv()
+    arrive(o_copies)
+    for g in range(nf):
+        out[:, g * wide : (g + 1) * wide] = ow[g]
+    arrive(gg_copies)
     gfin[y] = summed(gg)
     ga_copies = share(gfin, y, over_y, gas, gar)
-    relay(4, 0, None)
-    relay(4, 1, None)
+    for j in range(CUTS):
+        relay(4, j, None)
     remote_back(2, 4)
     remote_back(3, 5)
-    for copy in ga_copies:
-        copy.wait_recv()
+    arrive(ga_copies)
     result = gfin[...].reshape(2 * width, gfin.shape[2]).astype(F32)
     gs[...] = result[:width]
     gn[...] = result[width:]
@@ -505,16 +503,11 @@
 
 
 def write_out(*refs):
-    ins, outs, held, sems = refs[:4], refs[4:8], refs[8:12], refs[12]
-    fetch = [pltpu.make_async_copy(ins[k], held[k], sems.at[0, k]) for k in range(4)]
-    store = [pltpu.make_async_copy(held[k], outs[k], sems.at[1, k]) for k in range(4)]
-    for k in range(4):
-        fetch[k].start()
-    for k in range(4):
-        fetch[k].wait()
-        store[k].start()
-    for k in range(4):
-        store[k].wait()
+    copies = [pltpu.make_async_copy(refs[k], refs[4 + k], refs[8].at[k]) for k in range(4)]
+    for copy in copies:
+        copy.start()
+    for copy in copies:
+        copy.wait()
 
 
 def body(
@@ -621,16 +614,16 @@
             dma((ny,)),
         ],
         compiler_params=pltpu.CompilerParams(
-            collective_id=0, has_side_effects=True, vmem_limit_bytes=60 * 1024 * 1024
+            collective_id=0, has_side_effects=True, vmem_limit_bytes=32 * 1024 * 1024
         ),
-    )(*args)
+    )(*[pltpu.with_memory_space_constraint(a, pltpu.HBM) for a in args])
     out, gx, gs, gn = pl.pallas_call(
         write_out,
         out_shape=tuple(jax.ShapeDtypeStruct(r.shape, r.dtype) for r in results),
-        in_specs=[hbm] * 4,
+        in_specs=[vmem] * 4,
         out_specs=(hbm,) * 4,
-        scratch_shapes=[pltpu.VMEM(r.shape, r.dtype) for r in results] + [dma((2, 4))],
-        compiler_params=pltpu.CompilerParams(vmem_limit_bytes=60 * 1024 * 1024),
+        scratch_shapes=[dma((4,))],
+        compiler_params=pltpu.CompilerParams(vmem_limit_bytes=16 * 1024 * 1024),
     )(*results)
     return out.T, gx.T, gs, gn
 

time: 89.8 us -> 86.4 us (0.962)
  Pallas kernels: 89 us -> 85.5 us
    pallas_call x1, Pallas kernels: 87.1 us -> 84.6 us  [body(): pl.pallas_call(functools.partial(kernel, nd, nf, offsets), out_shape=(jax...]
    pallas_call x1, Pallas kernels: 1.88 us -> 0.87 us  [body(): pl.pallas_call(write_out, out_shape=tuple((jax.ShapeDtypeStruct(r.shape,...]
where the time goes in v5:
time: 86.4 us; the launch traced here: 86.1 us
  Pallas kernels  85.5 us (99%)
    pallas_call x1, Pallas kernels, body(): pl.pallas_call(functools.partial(kernel, nd, nf, offsets), out_shape=(jax...  84.6 us

profile of v5, /device:TPU:1, one launch (start us, length us, event | category | flops | bytes accessed | tf_op | source)
XLA Modules:
  0.0 86.1 jit_solution(8349955369139498405)
XLA Ops:
  0.6 84.6 %shard_map.138 = (bf16[64,1024]{1,0:T(8,128)(2,1)S(1)}, f32[64,1024]{1,0:T(8,128)S(1)}, f32[64,512]{1,0:T(8,128)S(1)}, f32[64,512]{1,0:T(8,128)S(1)}) custom-call(s32[1,16]{1,0:T(1,128)} %refs_0_.1, s32[1,16]{1,0:T(1,128)} %refs_1_.1, s32[6,1,8]{2,1,0:T(1,128)} %bitcast.14, s32[6,1,8]{2,1,0:T(1,128)} %bitcast.15, bf16[64,1024]{1,0:T(8,128)(2,1)} %bitcast.11, ...), custom_call_target="tpu_custom_call" | custom-call | tf_op jit(solution)/shard_map/pallas_call | solution.py:553
  85.2 0.9 %shard_map.139 = (bf16[64,1024]{1,0:T(8,128)(2,1)}, f32[64,1024]{1,0:T(8,128)}, f32[64,512]{1,0:T(8,128)}, f32[64,512]{1,0:T(8,128)}) custom-call(bf16[64,1024]{1,0:T(8,128)(2,1)S(1)} %get-tuple-element.12.refs_0_, f32[64,1024]{1,0:T(8,128)S(1)} %get-tuple-element.13.refs_1_, f32[64,512]{1,0:T(8,128)S(1)} %get-tuple-element.14.refs_2_, ...), custom_call_target="tpu_custom_call" | custom-call | tf_op jit(solution)/shard_map/pallas_call | solution.py:620

commit v6 on v5

--- a/solution.py
+++ b/solution.py
@@ -473,11 +473,12 @@
     gz_copies = share(gz, zl, in_group, gzs, gzr)
     remote_back(0, 0)
     remote_back(5, 1)
-    for j in range(CUTS):
-        relay(2, j, second)
+    relay(2, 0, second)
     arrive(gz_copies)
     gg[zg] = summed(gz)
     gg_copies = share(gg, zg, over_groups, ggs, ggr)
+    for j in range(1, CUTS):
+        relay(2, j, second)
     remote_back(1, 2)
     remote_back(4, 3)
     arrive(o_copies)

time: 86.4 us -> 85.5 us (0.990); the launches traced: 86.1 us -> 84.2 us
  Pallas kernels: 85.5 us -> 83.6 us
    pallas_call x1, Pallas kernels: 84.6 us -> 82.7 us  [body(): pl.pallas_call(functools.partial(kernel, nd, nf, offsets), out_shape=(jax...]
where the time goes in v6:
time: 85.5 us; the launch traced here: 84.2 us
  Pallas kernels  83.6 us (98%)
    pallas_call x1, Pallas kernels, body(): pl.pallas_call(functools.partial(kernel, nd, nf, offsets), out_shape=(jax...  82.7 us

profile of v6, /device:TPU:1, one launch (start us, length us, event | category | flops | bytes accessed | tf_op | source)
XLA Modules:
  0.0 84.2 jit_solution(1326060241941724996)
XLA Ops:
  0.6 82.7 %shard_map.138 = (bf16[64,1024]{1,0:T(8,128)(2,1)S(1)}, f32[64,1024]{1,0:T(8,128)S(1)}, f32[64,512]{1,0:T(8,128)S(1)}, f32[64,512]{1,0:T(8,128)S(1)}) custom-call(s32[1,16]{1,0:T(1,128)} %refs_0_.1, s32[1,16]{1,0:T(1,128)} %refs_1_.1, s32[6,1,8]{2,1,0:T(1,128)} %bitcast.14, s32[6,1,8]{2,1,0:T(1,128)} %bitcast.15, bf16[64,1024]{1,0:T(8,128)(2,1)} %bitcast.11, ...), custom_call_target="tpu_custom_call" | custom-call | tf_op jit(solution)/shard_map/pallas_call | solution.py:554
  83.4 0.9 %shard_map.139 = (bf16[64,1024]{1,0:T(8,128)(2,1)}, f32[64,1024]{1,0:T(8,128)}, f32[64,512]{1,0:T(8,128)}, f32[64,512]{1,0:T(8,128)}) custom-call(bf16[64,1024]{1,0:T(8,128)(2,1)S(1)} %get-tuple-element.12.refs_0_, f32[64,1024]{1,0:T(8,128)S(1)} %get-tuple-element.13.refs_1_, f32[64,512]{1,0:T(8,128)S(1)} %get-tuple-element.14.refs_2_, ...), custom_call_target="tpu_custom_call" | custom-call | tf_op jit(solution)/shard_map/pallas_call | solution.py:621
